TPU v7x, 512 devices: a whole 4x4x16 slice. The times are simulated.
512 devices in a mesh: blk: 128 (over x, z_lo, y), rep: 4 (over z_hi, core).
Axes of the slice: x: 4, y: 4, z: 16 (z_hi: 2, z_lo: 8; z = z_hi * 8 + z_lo), core: 2. Of those that a mesh axis runs over, the one named last changes fastest.
Arguments:
- queries: bfloat16 [16384, 512], P('blk'), may hold values from -3.59375 to 3.59375
- keys: bfloat16 [16384, 128], P('blk'), may hold values from -6 to 6
- values: bfloat16 [16384, 128], P('blk'), may hold values from -6 to 6
- output: bfloat16 [16384, 512], P('blk'), may hold values from -6 to 6
- grad_out: bfloat16 [16384, 512], P('blk'), may hold values from -6 to 6
- lse: float32 [4, 16384], P(None, 'blk'), may hold values from -1 to 12.5
- positions: int32 [16384], P('blk'), may hold values from 0 to 1073741823, as said below
Outputs:
- grad_queries: bfloat16 [16384, 512], P('blk')
- grad_keys: bfloat16 [16384, 128], P('blk')
- grad_values: bfloat16 [16384, 128], P('blk')
Inputs may be any that keep to these rules, and one draw needn't show every extreme that they name: positions are distinct. A token's place is the number of tokens with a smaller key. Cut the places into 2 n blocks of 64 consecutive places, n = 128; the rows of each index of blk hold the places of block c in order and then those of block 2 n - 1 - c in order, with c drawn at random for each index, every c once.
All inputs are finite; a program needn't handle non-finite values.
Results may differ from a plain program's by a relative error of at most 0.005.
Values may be sent and summed in bfloat16 or wider, within the bound.
A program may use at most 64 MiB of HBM per device.

v0:
```python
import jax
import jax.numpy as jnp
from jax import lax
from jax.sharding import PartitionSpec as P


def shifted_2(shard, axis, by):
    devices = lax.axis_size(axis)
    return lax.ppermute(shard, axis, [(i, (i + by) % devices) for i in range(devices)])


def pair_terms(
    score_scale,
    query_part,
    grad_part,
    lse_part,
    delta_part,
    query_pos,
    key_part,
    value_part,
    key_pos,
):
    scores = (
        jnp.einsum("pthd,pkd->phtk", query_part, key_part, preferred_element_type=jnp.float32)
        * score_scale
    )
    visible = key_pos[:, None, None, :] <= query_pos[:, None, :, None]
    probs = jnp.where(visible, jnp.exp(scores - lse_part[:, :, :, None]), 0.0)
    probs_low = probs.astype(jnp.bfloat16)
    value_terms = jnp.einsum(
        "phtk,pthd->pkd", probs_low, grad_part, preferred_element_type=jnp.float32
    )
    grad_probs = jnp.einsum(
        "pthd,pkd->phtk", grad_part, value_part, preferred_element_type=jnp.float32
    )
    grad_scores = (probs * (grad_probs - delta_part[:, :, :, None]) * score_scale).astype(
        jnp.bfloat16
    )
    query_terms = jnp.einsum(
        "phtk,pkd->pthd", grad_scores, key_part, preferred_element_type=jnp.float32
    )
    key_terms = jnp.einsum(
        "phtk,pthd->pkd", grad_scores, query_part, preferred_element_type=jnp.float32
    )
    pair_count = query_part.shape[0]
    part_rows = query_part.shape[1]
    return (query_terms.reshape(pair_count, part_rows, -1), key_terms, value_terms)


def moved(pair, amount):
    return shifted_2((pair[0], pair[1]), "blk", amount)


def carried(pair, amount):
    return shifted_2((pair[0], pair[1]), "blk", amount)


def pick(flags, first, second):
    shape = (flags.shape[0],) + (1,) * (first.ndim - 1)
    return jnp.where(flags.reshape(shape), first, second)


def per_device(queries, keys, values, output, grad_out, lse, positions):
    cycle_size = lax.axis_size("blk")
    group_size = lax.axis_size("rep")
    cycle_pos = lax.axis_index("blk")
    group = lax.axis_index("rep")
    tok_rows = keys.shape[0]
    half_rows = tok_rows // 2
    head_dim = keys.shape[1]
    head_count = queries.shape[1] // head_dim
    score_scale = head_dim ** (-0.5)
    quarter = cycle_size // group_size
    limit = 4
    window = min(limit, quarter)
    turn_count = quarter // window
    bit_count = group_size.bit_length() - 1
    query_heads = queries.reshape(tok_rows, head_count, head_dim)
    grad_heads = grad_out.reshape(tok_rows, head_count, head_dim)
    out_heads = output.reshape(tok_rows, head_count, head_dim)
    row_delta = jnp.sum(grad_heads.astype(jnp.float32) * out_heads.astype(jnp.float32), axis=2).T
    everyone = lax.all_gather(positions, "blk", axis=0, tiled=True).reshape(cycle_size, tok_rows)
    query_lo = query_heads[:half_rows]
    query_hi = query_heads[half_rows:]
    grad_lo = grad_heads[:half_rows]
    grad_hi = grad_heads[half_rows:]
    lse_lo = lse[:, :half_rows]
    lse_hi = lse[:, half_rows:]
    delta_lo = row_delta[:, :half_rows]
    delta_hi = row_delta[:, half_rows:]
    qpos_lo = positions[:half_rows]
    qpos_hi = positions[half_rows:]
    start_pair = (keys, values)
    for place in range(bit_count):
        shifted = moved(start_pair, quarter << place)
        chosen = group >> place & 1 == 1
        start_pair = (
            jnp.where(chosen, shifted[0], start_pair[0]),
            jnp.where(chosen, shifted[1], start_pair[1]),
        )
    win_keys = start_pair[0][None]
    win_values = start_pair[1][None]
    filled = 1
    while filled < window:
        step = min(filled, window - filled)
        extra = moved((win_keys, win_values), filled)
        win_keys = jnp.concatenate([win_keys, extra[0]], axis=0)
        win_values = jnp.concatenate([win_values, extra[1]], axis=0)
        filled = filled + step
    own_terms = pair_terms(
        score_scale,
        query_lo[None],
        grad_lo[None],
        lse_lo[None],
        delta_lo[None],
        qpos_lo[None],
        keys[:half_rows][None],
        values[:half_rows][None],
        qpos_lo[None],
    )
    own_weight = jnp.where(group == 0, 1.0, 0.0).astype(jnp.float32)
    grad_keys = jnp.zeros((window, tok_rows, head_dim), jnp.float32)
    grad_values = jnp.zeros((window, tok_rows, head_dim), jnp.float32)
    grad_query = jnp.zeros((tok_rows, head_count * head_dim), jnp.float32)
    members = jnp.arange(window, dtype=jnp.int32)

    def one_turn(turn, carry):
        win_keys, win_values, grad_keys, grad_values, grad_query = carry
        owners = (cycle_pos - quarter * group - members - window * turn) % cycle_size
        owner_pos = everyone[owners]
        lower = owner_pos[:, 0] < positions[0]
        key_lo = win_keys[:, :half_rows]
        key_hi = win_keys[:, half_rows:]
        value_lo = win_values[:, :half_rows]
        value_hi = win_values[:, half_rows:]
        kpos_lo = owner_pos[:, :half_rows]
        kpos_hi = owner_pos[:, half_rows:]
        pair_shape = (window * 2,)
        query_pair = jnp.stack(
            [
                jnp.broadcast_to(query_hi, (window,) + query_hi.shape),
                pick(
                    lower,
                    jnp.broadcast_to(query_lo, (window,) + query_lo.shape),
                    jnp.broadcast_to(query_hi, (window,) + query_hi.shape),
                ),
            ],
            axis=1,
        )
        grad_pair = jnp.stack(
            [
                jnp.broadcast_to(grad_hi, (window,) + grad_hi.shape),
                pick(
                    lower,
                    jnp.broadcast_to(grad_lo, (window,) + grad_lo.shape),
                    jnp.broadcast_to(grad_hi, (window,) + grad_hi.shape),
                ),
            ],
            axis=1,
        )
        lse_pair = jnp.stack(
            [
                jnp.broadcast_to(lse_hi, (window,) + lse_hi.shape),
                pick(
                    lower,
                    jnp.broadcast_to(lse_lo, (window,) + lse_lo.shape),
                    jnp.broadcast_to(lse_hi, (window,) + lse_hi.shape),
                ),
            ],
            axis=1,
        )
        delta_pair = jnp.stack(
            [
                jnp.broadcast_to(delta_hi, (window,) + delta_hi.shape),
                pick(
                    lower,
                    jnp.broadcast_to(delta_lo, (window,) + delta_lo.shape),
                    jnp.broadcast_to(delta_hi, (window,) + delta_hi.shape),
                ),
            ],
            axis=1,
        )
        qpos_pair = jnp.stack(
            [
                jnp.broadcast_to(qpos_hi, (window, half_rows)),
                pick(
                    lower,
                    jnp.broadcast_to(qpos_lo, (window, half_rows)),
                    jnp.broadcast_to(qpos_hi, (window, half_rows)),
                ),
            ],
            axis=1,
        )
        key_pair = jnp.stack([key_lo, pick(lower, key_lo, key_hi)], axis=1)
        value_pair = jnp.stack([value_lo, pick(lower, value_lo, value_hi)], axis=1)
        kpos_pair = jnp.stack([kpos_lo, pick(lower, kpos_lo, kpos_hi)], axis=1)
        terms = pair_terms(
            score_scale,
            query_pair.reshape(pair_shape + query_pair.shape[2:]),
            grad_pair.reshape(pair_shape + grad_pair.shape[2:]),
            lse_pair.reshape(pair_shape + lse_pair.shape[2:]),
            delta_pair.reshape(pair_shape + delta_pair.shape[2:]),
            qpos_pair.reshape(pair_shape + qpos_pair.shape[2:]),
            key_pair.reshape(pair_shape + key_pair.shape[2:]),
            value_pair.reshape(pair_shape + value_pair.shape[2:]),
            kpos_pair.reshape(pair_shape + kpos_pair.shape[2:]),
        )
        query_terms = terms[0].reshape(window, 2, half_rows, head_count * head_dim)
        key_terms = terms[1].reshape(window, 2, half_rows, head_dim)
        value_terms = terms[2].reshape(window, 2, half_rows, head_dim)
        zeros_query = jnp.zeros_like(query_terms[:, 1])
        add_lo = jnp.sum(pick(lower, query_terms[:, 1], zeros_query), axis=0)
        add_hi = jnp.sum(query_terms[:, 0], axis=0) + jnp.sum(
            pick(lower, zeros_query, query_terms[:, 1]), axis=0
        )
        grad_query = grad_query + jnp.concatenate([add_lo, add_hi], axis=0)
        zeros_key = jnp.zeros_like(key_terms[:, 1])
        key_add = jnp.concatenate(
            [
                key_terms[:, 0] + pick(lower, key_terms[:, 1], zeros_key),
                pick(lower, zeros_key, key_terms[:, 1]),
            ],
            axis=1,
        )
        value_add = jnp.concatenate(
            [
                value_terms[:, 0] + pick(lower, value_terms[:, 1], zeros_key),
                pick(lower, zeros_key, value_terms[:, 1]),
            ],
            axis=1,
        )
        grad_keys = grad_keys + key_add
        grad_values = grad_values + value_add
        win_keys, win_values = shifted_2((win_keys, win_values), "blk", window)
        grad_keys, grad_values = shifted_2((grad_keys, grad_values), "blk", window)
        return (win_keys, win_values, grad_keys, grad_values, grad_query)

    final = lax.fori_loop(
        0, turn_count, one_turn, (win_keys, win_values, grad_keys, grad_values, grad_query)
    )
    grad_keys = final[2]
    grad_values = final[3]
    grad_query = final[4]
    count = window
    while count > 1:
        lead = (count + 1) // 2
        extra = carried((grad_keys[lead:count], grad_values[lead:count]), -lead)
        tail = count - lead
        grad_keys = jnp.concatenate([grad_keys[:tail] + extra[0], grad_keys[tail:lead]], axis=0)
        grad_values = jnp.concatenate(
            [grad_values[:tail] + extra[1], grad_values[tail:lead]], axis=0
        )
        count = lead
    total_keys = grad_keys[0]
    total_values = grad_values[0]
    remaining = group_size - 1 - group
    for place in range(bit_count):
        shifted = carried((total_keys, total_values), quarter << place)
        chosen = remaining >> place & 1 == 1
        total_keys = jnp.where(chosen, shifted[0], total_keys)
        total_values = jnp.where(chosen, shifted[1], total_values)
    own_pad = jnp.zeros((half_rows, head_dim), jnp.float32)
    total_keys = total_keys + own_weight * jnp.concatenate([own_terms[1][0], own_pad], axis=0)
    total_values = total_values + own_weight * jnp.concatenate([own_terms[2][0], own_pad], axis=0)
    grad_query = grad_query + own_weight * jnp.concatenate(
        [own_terms[0][0], jnp.zeros((half_rows, head_count * head_dim), jnp.float32)], axis=0
    )
    summed = lax.psum((grad_query, total_keys, total_values), "rep")
    return (
        summed[0].astype(jnp.bfloat16),
        summed[1].astype(jnp.bfloat16),
        summed[2].astype(jnp.bfloat16),
    )


def solution(mesh):
    placed = (
        P("blk", None),
        P("blk", None),
        P("blk", None),
        P("blk", None),
        P("blk", None),
        P(None, "blk"),
        P("blk"),
    )
    return jax.shard_map(
        per_device,
        mesh=mesh,
        in_specs=placed,
        out_specs=(P("blk", None), P("blk", None), P("blk", None)),
        check_vma=False,
    )
```

profile of v0, /device:TPU:1, one launch (start us, length us, event | category | flops | bytes accessed | tf_op | source)
XLA Modules:
  0.0 908.9 jit_solution(14726433039888393091)
XLA Ops:
  0.6 3.9 collective-permute-start.4
  4.6 3.1 collective-permute-start.8
  15.2 469.5 %all-gather = s32[128,1,128]{2,1,0:T(1,128)S(1)} all-gather(s32[1,1,128]{2,1,0:T(1,128)S(1)} %bitcast.269), channel_id=1, replica_groups=mesh['blk'=128,'rep'=4] {'blk'}, dimensions={0}, use_global_device_ids=true | all-gather | bytes 66048 | tf_op jit(solution)/shard_map/all_gather | solution.py:82
  484.7 1.9 collective-permute-start.5
  486.7 4.9 collective-permute-start.9
  491.6 1.9 collective-permute-start.6
  493.5 1.9 collective-permute-start.10
  495.4 11.6 %collective-permute-done.6 = bf16[1,128,128]{2,1,0:T(8,128)(2,1)S(1)} collective-permute-done((bf16[1,128,128]{2,1,0:T(8,128)(2,1)S(1)}, bf16[1,128,128]{2,1,0:T(8,128)(2,1)S(1)}, u32[]{:S(2)}, u32[]{:S(2)}) %collective-permute-start.6) | collective-permute-done | bytes 32800 | tf_op jit(solution)/shard_map/ppermute | solution.py:9
  507.1 1.9 collective-permute-start.7
  509.0 1.9 collective-permute-start.11
  510.9 12.2 %collective-permute-done.7 = bf16[2,128,128]{2,1,0:T(8,128)(2,1)S(1)} collective-permute-done((bf16[2,128,128]{2,1,0:T(8,128)(2,1)S(1)}, bf16[2,128,128]{2,1,0:T(8,128)(2,1)S(1)}, u32[]{:S(2)}, u32[]{:S(2)}) %collective-permute-start.7) | collective-permute-done | bytes 65568 | tf_op jit(solution)/shard_map/ppermute | solution.py:9
  525.9 245.9 %while.24 = (s32[]{:T(128)}, bf16[4,128,128]{2,1,0:T(8,128)(2,1)}, bf16[4,128,128]{2,1,0:T(8,128)(2,1)}, f32[4,128,128]{2,1,0:T(8,128)S(1)}, f32[4,128,128]{2,1,...) while((s32[]{:T(128)}, bf16[4,128,128]{2,1,0:T(8,128)(2,1)}, ...), condition=%wide.region_5.6_spmd.clone, body=%wide.region_1.5_spmd.clone.sunk | while | flops 171090496 | bytes 26398304 | solution.py:238
  535.3 1.9 collective-permute-start.2
  541.7 2.5 collective-permute-done.1
  544.2 7.5 collective-permute-done.2
  551.7 2.8 collective-permute-done.3
  564.6 1.9 collective-permute-start.2
  571.0 2.5 collective-permute-done.1
  573.5 7.0 collective-permute-done.2
  580.5 2.9 collective-permute-done.3
  599.9 3.9 collective-permute-done.1
  603.8 5.9 collective-permute-done.2
  609.7 5.6 collective-permute-done.3
  631.9 3.4 collective-permute-done.1
  635.3 6.0 collective-permute-done.2
  641.3 5.3 collective-permute-done.3
  656.7 1.9 collective-permute-start.2
  663.1 2.5 collective-permute-done.1
  665.6 7.1 collective-permute-done.2
  672.7 4.5 collective-permute-done.3
  693.7 2.5 collective-permute-done.1
  696.2 7.8 collective-permute-done.2
  704.0 4.5 collective-permute-done.3
  725.0 2.5 collective-permute-done.1
  727.5 7.8 collective-permute-done.2
  735.3 4.5 collective-permute-done.3
  756.3 2.5 collective-permute-done.1
  758.8 7.9 collective-permute-done.2
  766.7 4.4 collective-permute-done.3
  771.8 2.1 collective-permute-start.12
  773.9 7.4 collective-permute-start.16
  781.4 1.9 collective-permute-start.13
  783.6 9.5 %collective-permute-start.17 = (f32[1,128,128]{2,1,0:T(8,128)S(1)}, f32[1,128,128]{2,1,0:T(8,128)S(1)}, u32[]{:S(2)}, u32[]{:S(2)}) collective-permute-start(f32[1,128,128]{2,1,0:T(8,128)S(1)} %slice.266), channel_id=1, source_target_pairs={{0,508},{4,0},{8,4},{12,8},{16,12},{20,16},{24,20},{28,24},{32,28}... | collective-permute-start | bytes 196616 | tf_op jit(solution)/shard_map/ppermute | solution.py:9
  797.0 2.6 collective-permute-done.14
  799.7 3.1 collective-permute-start.15
  802.8 3.7 collective-permute-done.18
  808.6 4.5 collective-permute-done.19
  813.1 95.8 %all-reduce.5 = (bf16[128,512]{1,0:T(8,128)(2,1)}, bf16[128,128]{1,0:T(8,128)(2,1)}, bf16[128,128]{1,0:T(8,128)(2,1)}) all-reduce(f32[128,512]{1,0:T(8,128)S(1)} %multiply_add_fusion, f32[128,128]{1,0:T(8,128)S(1)} %multiply_add_fusion.2, f32[128,128]{1,0:T(8,128)S(1)} %multiply_add_fusion.1), channel_id=1, replica_groups=mesh['blk'=128,'rep'=4] {'rep'}, use_global_device_ids=true, to_apply=%region_6.7 | all-reduce | flops 98304 | bytes 589824 | tf_op jit(solution)/shard_map/psum | solution.py:268
  (641 shorter events, 140.0 us)
Async XLA Ops:
  0.6 484.1 %collective-permute-start.4 = (bf16[128,128]{1,0:T(8,128)(2,1)}, bf16[128,128]{1,0:T(8,128)(2,1)S(1)}, u32[]{:S(2)}, u32[]{:S(2)}) collective-permute-start(bf16[128,128]{1,0:T(8,128)(2,1)} %param.10), channel_id=1, source_target_pairs={{0,128},{4,132},{8,136},{12,140},{16,144},{20,148},{24,152},{28,15... | collective-permute-start | bytes 98312 | tf_op jit(solution)/shard_map/ppermute | solution.py:9
  4.6 482.1 %collective-permute-start.8 = (bf16[128,128]{1,0:T(8,128)(2,1)}, bf16[128,128]{1,0:T(8,128)(2,1)S(1)}, u32[]{:S(2)}, u32[]{:S(2)}) collective-permute-start(bf16[128,128]{1,0:T(8,128)(2,1)} %param.11), channel_id=1, source_target_pairs={{0,128},{4,132},{8,136},{12,140},{16,144},{20,148},{24,152},{28,15... | collective-permute-start | bytes 98312 | tf_op jit(solution)/shard_map/ppermute | solution.py:9
  484.7 6.8 collective-permute-start.5
  486.7 6.8 collective-permute-start.9
  491.6 15.5 %collective-permute-start.6 = (bf16[1,128,128]{2,1,0:T(8,128)(2,1)S(1)}, bf16[1,128,128]{2,1,0:T(8,128)(2,1)S(1)}, u32[]{:S(2)}, u32[]{:S(2)}) collective-permute-start(bf16[1,128,128]{2,1,0:T(8,128)(2,1)S(1)} %select_bitcast_fusion.4), channel_id=1, source_target_pairs={{0,4},{4,8},{8,12},{12,16},{16,20},{20,24},{24,28},{28,32},{32,36}... | collective-permute-start | bytes 98312 | tf_op jit(solution)/shard_map/ppermute | solution.py:9
  493.5 15.5 %collective-permute-start.10 = (bf16[1,128,128]{2,1,0:T(8,128)(2,1)S(1)}, bf16[1,128,128]{2,1,0:T(8,128)(2,1)S(1)}, u32[]{:S(2)}, u32[]{:S(2)}) collective-permute-start(bf16[1,128,128]{2,1,0:T(8,128)(2,1)S(1)} %select_bitcast_fusion.3), channel_id=1, source_target_pairs={{0,4},{4,8},{8,12},{12,16},{16,20},{20,24},{24,28},{28,32},{32,36}... | collective-permute-start | bytes 98312 | tf_op jit(solution)/shard_map/ppermute | solution.py:9
  507.1 16.1 %collective-permute-start.7 = (bf16[2,128,128]{2,1,0:T(8,128)(2,1)S(1)}, bf16[2,128,128]{2,1,0:T(8,128)(2,1)S(1)}, u32[]{:S(2)}, u32[]{:S(2)}) collective-permute-start(bf16[2,128,128]{2,1,0:T(8,128)(2,1)S(1)} %pad_maximum_fusion.8), channel_id=1, source_target_pairs={{0,8},{4,12},{8,16},{12,20},{16,24},{20,28},{24,32},{28,36},{32,40... | collective-permute-start | bytes 196616 | tf_op jit(solution)/shard_map/ppermute | solution.py:9
  509.0 16.1 %collective-permute-start.11 = (bf16[2,128,128]{2,1,0:T(8,128)(2,1)S(1)}, bf16[2,128,128]{2,1,0:T(8,128)(2,1)S(1)}, u32[]{:S(2)}, u32[]{:S(2)}) collective-permute-start(bf16[2,128,128]{2,1,0:T(8,128)(2,1)S(1)} %pad_maximum_fusion.9), channel_id=1, source_target_pairs={{0,8},{4,12},{8,16},{12,20},{16,24},{20,28},{24,32},{28,36},{32,40... | collective-permute-start | bytes 196616 | tf_op jit(solution)/shard_map/ppermute | solution.py:9
  526.9 14.9 %collective-permute-start = (bf16[4,128,128]{2,1,0:T(8,128)(2,1)S(1)}, bf16[4,128,128]{2,1,0:T(8,128)(2,1)}, u32[]{:S(2)}, u32[]{:S(2)}) collective-permute-start(bf16[4,128,128]{2,1,0:T(8,128)(2,1)S(1)} %copy.99), channel_id=1, source_target_pairs={{0,16},{4,20},{8,24},{12,28},{16,32},{20,36},{24,40},{28,44},{32,4... | collective-permute-start | bytes 393224 | tf_op jit(solution)/shard_map/while/body/eval_jaxpr/ppermute | solution.py:9
  529.7 14.5 %collective-permute-start.1 = (bf16[4,128,128]{2,1,0:T(8,128)(2,1)S(1)}, bf16[4,128,128]{2,1,0:T(8,128)(2,1)}, u32[]{:S(2)}, u32[]{:S(2)}) collective-permute-start(bf16[4,128,128]{2,1,0:T(8,128)(2,1)S(1)} %copy.100), channel_id=1, source_target_pairs={{0,16},{4,20},{8,24},{12,28},{16,32},{20,36},{24,40},{28,44},{32,4... | collective-permute-start | bytes 393224 | tf_op jit(solution)/shard_map/while/body/eval_jaxpr/ppermute | solution.py:9
  535.3 16.3 %collective-permute-start.2 = (f32[4,128,128]{2,1,0:T(8,128)S(1)}, f32[4,128,128]{2,1,0:T(8,128)S(1)}, u32[]{:S(2)}, u32[]{:S(2)}) collective-permute-start(f32[4,128,128]{2,1,0:T(8,128)S(1)} %maximum_add_fusion.6), channel_id=1, source_target_pairs={{0,16},{4,20},{8,24},{12,28},{16,32},{20,36},{24,40},{28,44},{32,4... | collective-permute-start | bytes 786440 | tf_op jit(solution)/shard_map/while/body/eval_jaxpr/ppermute | solution.py:9
  538.0 16.5 %collective-permute-start.3 = (f32[4,128,128]{2,1,0:T(8,128)}, f32[4,128,128]{2,1,0:T(8,128)S(1)}, u32[]{:S(2)}, u32[]{:S(2)}) collective-permute-start(f32[4,128,128]{2,1,0:T(8,128)} %maximum_add_fusion.7), channel_id=1, source_target_pairs={{0,16},{4,20},{8,24},{12,28},{16,32},{20,36},{24,40},{28,44},{32,4... | collective-permute-start | bytes 786440 | tf_op jit(solution)/shard_map/while/body/eval_jaxpr/ppermute | solution.py:9
  556.2 14.9 %collective-permute-start = (bf16[4,128,128]{2,1,0:T(8,128)(2,1)S(1)}, bf16[4,128,128]{2,1,0:T(8,128)(2,1)}, u32[]{:S(2)}, u32[]{:S(2)}) collective-permute-start(bf16[4,128,128]{2,1,0:T(8,128)(2,1)S(1)} %copy.99), channel_id=1, source_target_pairs={{0,16},{4,20},{8,24},{12,28},{16,32},{20,36},{24,40},{28,44},{32,4... | collective-permute-start | bytes 393224 | tf_op jit(solution)/shard_map/while/body/eval_jaxpr/ppermute | solution.py:9
  559.0 14.5 %collective-permute-start.1 = (bf16[4,128,128]{2,1,0:T(8,128)(2,1)S(1)}, bf16[4,128,128]{2,1,0:T(8,128)(2,1)}, u32[]{:S(2)}, u32[]{:S(2)}) collective-permute-start(bf16[4,128,128]{2,1,0:T(8,128)(2,1)S(1)} %copy.100), channel_id=1, source_target_pairs={{0,16},{4,20},{8,24},{12,28},{16,32},{20,36},{24,40},{28,44},{32,4... | collective-permute-start | bytes 393224 | tf_op jit(solution)/shard_map/while/body/eval_jaxpr/ppermute | solution.py:9
  564.6 15.8 %collective-permute-start.2 = (f32[4,128,128]{2,1,0:T(8,128)S(1)}, f32[4,128,128]{2,1,0:T(8,128)S(1)}, u32[]{:S(2)}, u32[]{:S(2)}) collective-permute-start(f32[4,128,128]{2,1,0:T(8,128)S(1)} %maximum_add_fusion.6), channel_id=1, source_target_pairs={{0,16},{4,20},{8,24},{12,28},{16,32},{20,36},{24,40},{28,44},{32,4... | collective-permute-start | bytes 786440 | tf_op jit(solution)/shard_map/while/body/eval_jaxpr/ppermute | solution.py:9
  567.3 16.0 %collective-permute-start.3 = (f32[4,128,128]{2,1,0:T(8,128)}, f32[4,128,128]{2,1,0:T(8,128)S(1)}, u32[]{:S(2)}, u32[]{:S(2)}) collective-permute-start(f32[4,128,128]{2,1,0:T(8,128)} %maximum_add_fusion.7), channel_id=1, source_target_pairs={{0,16},{4,20},{8,24},{12,28},{16,32},{20,36},{24,40},{28,44},{32,4... | collective-permute-start | bytes 786440 | tf_op jit(solution)/shard_map/while/body/eval_jaxpr/ppermute | solution.py:9
  585.0 14.9 %collective-permute-start = (bf16[4,128,128]{2,1,0:T(8,128)(2,1)S(1)}, bf16[4,128,128]{2,1,0:T(8,128)(2,1)}, u32[]{:S(2)}, u32[]{:S(2)}) collective-permute-start(bf16[4,128,128]{2,1,0:T(8,128)(2,1)S(1)} %copy.99), channel_id=1, source_target_pairs={{0,16},{4,20},{8,24},{12,28},{16,32},{20,36},{24,40},{28,44},{32,4... | collective-permute-start | bytes 393224 | tf_op jit(solution)/shard_map/while/body/eval_jaxpr/ppermute | solution.py:9
  587.8 16.0 %collective-permute-start.1 = (bf16[4,128,128]{2,1,0:T(8,128)(2,1)S(1)}, bf16[4,128,128]{2,1,0:T(8,128)(2,1)}, u32[]{:S(2)}, u32[]{:S(2)}) collective-permute-start(bf16[4,128,128]{2,1,0:T(8,128)(2,1)S(1)} %copy.100), channel_id=1, source_target_pairs={{0,16},{4,20},{8,24},{12,28},{16,32},{20,36},{24,40},{28,44},{32,4... | collective-permute-start | bytes 393224 | tf_op jit(solution)/shard_map/while/body/eval_jaxpr/ppermute | solution.py:9
  593.5 16.2 %collective-permute-start.2 = (f32[4,128,128]{2,1,0:T(8,128)S(1)}, f32[4,128,128]{2,1,0:T(8,128)S(1)}, u32[]{:S(2)}, u32[]{:S(2)}) collective-permute-start(f32[4,128,128]{2,1,0:T(8,128)S(1)} %maximum_add_fusion.6), channel_id=1, source_target_pairs={{0,16},{4,20},{8,24},{12,28},{16,32},{20,36},{24,40},{28,44},{32,4... | collective-permute-start | bytes 786440 | tf_op jit(solution)/shard_map/while/body/eval_jaxpr/ppermute | solution.py:9
  596.2 19.2 %collective-permute-start.3 = (f32[4,128,128]{2,1,0:T(8,128)}, f32[4,128,128]{2,1,0:T(8,128)S(1)}, u32[]{:S(2)}, u32[]{:S(2)}) collective-permute-start(f32[4,128,128]{2,1,0:T(8,128)} %maximum_add_fusion.7), channel_id=1, source_target_pairs={{0,16},{4,20},{8,24},{12,28},{16,32},{20,36},{24,40},{28,44},{32,4... | collective-permute-start | bytes 786440 | tf_op jit(solution)/shard_map/while/body/eval_jaxpr/ppermute | solution.py:9
  617.0 14.9 %collective-permute-start = (bf16[4,128,128]{2,1,0:T(8,128)(2,1)S(1)}, bf16[4,128,128]{2,1,0:T(8,128)(2,1)}, u32[]{:S(2)}, u32[]{:S(2)}) collective-permute-start(bf16[4,128,128]{2,1,0:T(8,128)(2,1)S(1)} %copy.99), channel_id=1, source_target_pairs={{0,16},{4,20},{8,24},{12,28},{16,32},{20,36},{24,40},{28,44},{32,4... | collective-permute-start | bytes 393224 | tf_op jit(solution)/shard_map/while/body/eval_jaxpr/ppermute | solution.py:9
  619.8 15.5 %collective-permute-start.1 = (bf16[4,128,128]{2,1,0:T(8,128)(2,1)S(1)}, bf16[4,128,128]{2,1,0:T(8,128)(2,1)}, u32[]{:S(2)}, u32[]{:S(2)}) collective-permute-start(bf16[4,128,128]{2,1,0:T(8,128)(2,1)S(1)} %copy.100), channel_id=1, source_target_pairs={{0,16},{4,20},{8,24},{12,28},{16,32},{20,36},{24,40},{28,44},{32,4... | collective-permute-start | bytes 393224 | tf_op jit(solution)/shard_map/while/body/eval_jaxpr/ppermute | solution.py:9
  625.5 15.8 %collective-permute-start.2 = (f32[4,128,128]{2,1,0:T(8,128)S(1)}, f32[4,128,128]{2,1,0:T(8,128)S(1)}, u32[]{:S(2)}, u32[]{:S(2)}) collective-permute-start(f32[4,128,128]{2,1,0:T(8,128)S(1)} %maximum_add_fusion.6), channel_id=1, source_target_pairs={{0,16},{4,20},{8,24},{12,28},{16,32},{20,36},{24,40},{28,44},{32,4... | collective-permute-start | bytes 786440 | tf_op jit(solution)/shard_map/while/body/eval_jaxpr/ppermute | solution.py:9
  628.2 18.4 %collective-permute-start.3 = (f32[4,128,128]{2,1,0:T(8,128)}, f32[4,128,128]{2,1,0:T(8,128)S(1)}, u32[]{:S(2)}, u32[]{:S(2)}) collective-permute-start(f32[4,128,128]{2,1,0:T(8,128)} %maximum_add_fusion.7), channel_id=1, source_target_pairs={{0,16},{4,20},{8,24},{12,28},{16,32},{20,36},{24,40},{28,44},{32,4... | collective-permute-start | bytes 786440 | tf_op jit(solution)/shard_map/while/body/eval_jaxpr/ppermute | solution.py:9
  648.3 14.9 %collective-permute-start = (bf16[4,128,128]{2,1,0:T(8,128)(2,1)S(1)}, bf16[4,128,128]{2,1,0:T(8,128)(2,1)}, u32[]{:S(2)}, u32[]{:S(2)}) collective-permute-start(bf16[4,128,128]{2,1,0:T(8,128)(2,1)S(1)} %copy.99), channel_id=1, source_target_pairs={{0,16},{4,20},{8,24},{12,28},{16,32},{20,36},{24,40},{28,44},{32,4... | collective-permute-start | bytes 393224 | tf_op jit(solution)/shard_map/while/body/eval_jaxpr/ppermute | solution.py:9
  651.1 14.5 %collective-permute-start.1 = (bf16[4,128,128]{2,1,0:T(8,128)(2,1)S(1)}, bf16[4,128,128]{2,1,0:T(8,128)(2,1)}, u32[]{:S(2)}, u32[]{:S(2)}) collective-permute-start(bf16[4,128,128]{2,1,0:T(8,128)(2,1)S(1)} %copy.100), channel_id=1, source_target_pairs={{0,16},{4,20},{8,24},{12,28},{16,32},{20,36},{24,40},{28,44},{32,4... | collective-permute-start | bytes 393224 | tf_op jit(solution)/shard_map/while/body/eval_jaxpr/ppermute | solution.py:9
  656.7 15.9 %collective-permute-start.2 = (f32[4,128,128]{2,1,0:T(8,128)S(1)}, f32[4,128,128]{2,1,0:T(8,128)S(1)}, u32[]{:S(2)}, u32[]{:S(2)}) collective-permute-start(f32[4,128,128]{2,1,0:T(8,128)S(1)} %maximum_add_fusion.6), channel_id=1, source_target_pairs={{0,16},{4,20},{8,24},{12,28},{16,32},{20,36},{24,40},{28,44},{32,4... | collective-permute-start | bytes 786440 | tf_op jit(solution)/shard_map/while/body/eval_jaxpr/ppermute | solution.py:9
  659.4 17.7 %collective-permute-start.3 = (f32[4,128,128]{2,1,0:T(8,128)}, f32[4,128,128]{2,1,0:T(8,128)S(1)}, u32[]{:S(2)}, u32[]{:S(2)}) collective-permute-start(f32[4,128,128]{2,1,0:T(8,128)} %maximum_add_fusion.7), channel_id=1, source_target_pairs={{0,16},{4,20},{8,24},{12,28},{16,32},{20,36},{24,40},{28,44},{32,4... | collective-permute-start | bytes 786440 | tf_op jit(solution)/shard_map/while/body/eval_jaxpr/ppermute | solution.py:9
  678.9 14.9 %collective-permute-start = (bf16[4,128,128]{2,1,0:T(8,128)(2,1)S(1)}, bf16[4,128,128]{2,1,0:T(8,128)(2,1)}, u32[]{:S(2)}, u32[]{:S(2)}) collective-permute-start(bf16[4,128,128]{2,1,0:T(8,128)(2,1)S(1)} %copy.99), channel_id=1, source_target_pairs={{0,16},{4,20},{8,24},{12,28},{16,32},{20,36},{24,40},{28,44},{32,4... | collective-permute-start | bytes 393224 | tf_op jit(solution)/shard_map/while/body/eval_jaxpr/ppermute | solution.py:9
  681.7 14.5 %collective-permute-start.1 = (bf16[4,128,128]{2,1,0:T(8,128)(2,1)S(1)}, bf16[4,128,128]{2,1,0:T(8,128)(2,1)}, u32[]{:S(2)}, u32[]{:S(2)}) collective-permute-start(bf16[4,128,128]{2,1,0:T(8,128)(2,1)S(1)} %copy.100), channel_id=1, source_target_pairs={{0,16},{4,20},{8,24},{12,28},{16,32},{20,36},{24,40},{28,44},{32,4... | collective-permute-start | bytes 393224 | tf_op jit(solution)/shard_map/while/body/eval_jaxpr/ppermute | solution.py:9
  687.3 16.7 %collective-permute-start.2 = (f32[4,128,128]{2,1,0:T(8,128)S(1)}, f32[4,128,128]{2,1,0:T(8,128)S(1)}, u32[]{:S(2)}, u32[]{:S(2)}) collective-permute-start(f32[4,128,128]{2,1,0:T(8,128)S(1)} %maximum_add_fusion.6), channel_id=1, source_target_pairs={{0,16},{4,20},{8,24},{12,28},{16,32},{20,36},{24,40},{28,44},{32,4... | collective-permute-start | bytes 786440 | tf_op jit(solution)/shard_map/while/body/eval_jaxpr/ppermute | solution.py:9
  690.0 18.5 %collective-permute-start.3 = (f32[4,128,128]{2,1,0:T(8,128)}, f32[4,128,128]{2,1,0:T(8,128)S(1)}, u32[]{:S(2)}, u32[]{:S(2)}) collective-permute-start(f32[4,128,128]{2,1,0:T(8,128)} %maximum_add_fusion.7), channel_id=1, source_target_pairs={{0,16},{4,20},{8,24},{12,28},{16,32},{20,36},{24,40},{28,44},{32,4... | collective-permute-start | bytes 786440 | tf_op jit(solution)/shard_map/while/body/eval_jaxpr/ppermute | solution.py:9
  710.2 14.9 %collective-permute-start = (bf16[4,128,128]{2,1,0:T(8,128)(2,1)S(1)}, bf16[4,128,128]{2,1,0:T(8,128)(2,1)}, u32[]{:S(2)}, u32[]{:S(2)}) collective-permute-start(bf16[4,128,128]{2,1,0:T(8,128)(2,1)S(1)} %copy.99), channel_id=1, source_target_pairs={{0,16},{4,20},{8,24},{12,28},{16,32},{20,36},{24,40},{28,44},{32,4... | collective-permute-start | bytes 393224 | tf_op jit(solution)/shard_map/while/body/eval_jaxpr/ppermute | solution.py:9
  713.0 14.5 %collective-permute-start.1 = (bf16[4,128,128]{2,1,0:T(8,128)(2,1)S(1)}, bf16[4,128,128]{2,1,0:T(8,128)(2,1)}, u32[]{:S(2)}, u32[]{:S(2)}) collective-permute-start(bf16[4,128,128]{2,1,0:T(8,128)(2,1)S(1)} %copy.100), channel_id=1, source_target_pairs={{0,16},{4,20},{8,24},{12,28},{16,32},{20,36},{24,40},{28,44},{32,4... | collective-permute-start | bytes 393224 | tf_op jit(solution)/shard_map/while/body/eval_jaxpr/ppermute | solution.py:9
  718.6 16.7 %collective-permute-start.2 = (f32[4,128,128]{2,1,0:T(8,128)S(1)}, f32[4,128,128]{2,1,0:T(8,128)S(1)}, u32[]{:S(2)}, u32[]{:S(2)}) collective-permute-start(f32[4,128,128]{2,1,0:T(8,128)S(1)} %maximum_add_fusion.6), channel_id=1, source_target_pairs={{0,16},{4,20},{8,24},{12,28},{16,32},{20,36},{24,40},{28,44},{32,4... | collective-permute-start | bytes 786440 | tf_op jit(solution)/shard_map/while/body/eval_jaxpr/ppermute | solution.py:9
  721.3 18.5 %collective-permute-start.3 = (f32[4,128,128]{2,1,0:T(8,128)}, f32[4,128,128]{2,1,0:T(8,128)S(1)}, u32[]{:S(2)}, u32[]{:S(2)}) collective-permute-start(f32[4,128,128]{2,1,0:T(8,128)} %maximum_add_fusion.7), channel_id=1, source_target_pairs={{0,16},{4,20},{8,24},{12,28},{16,32},{20,36},{24,40},{28,44},{32,4... | collective-permute-start | bytes 786440 | tf_op jit(solution)/shard_map/while/body/eval_jaxpr/ppermute | solution.py:9
  741.5 14.9 %collective-permute-start = (bf16[4,128,128]{2,1,0:T(8,128)(2,1)S(1)}, bf16[4,128,128]{2,1,0:T(8,128)(2,1)}, u32[]{:S(2)}, u32[]{:S(2)}) collective-permute-start(bf16[4,128,128]{2,1,0:T(8,128)(2,1)S(1)} %copy.99), channel_id=1, source_target_pairs={{0,16},{4,20},{8,24},{12,28},{16,32},{20,36},{24,40},{28,44},{32,4... | collective-permute-start | bytes 393224 | tf_op jit(solution)/shard_map/while/body/eval_jaxpr/ppermute | solution.py:9
  744.3 14.5 %collective-permute-start.1 = (bf16[4,128,128]{2,1,0:T(8,128)(2,1)S(1)}, bf16[4,128,128]{2,1,0:T(8,128)(2,1)}, u32[]{:S(2)}, u32[]{:S(2)}) collective-permute-start(bf16[4,128,128]{2,1,0:T(8,128)(2,1)S(1)} %copy.100), channel_id=1, source_target_pairs={{0,16},{4,20},{8,24},{12,28},{16,32},{20,36},{24,40},{28,44},{32,4... | collective-permute-start | bytes 393224 | tf_op jit(solution)/shard_map/while/body/eval_jaxpr/ppermute | solution.py:9
  749.9 16.8 %collective-permute-start.2 = (f32[4,128,128]{2,1,0:T(8,128)S(1)}, f32[4,128,128]{2,1,0:T(8,128)S(1)}, u32[]{:S(2)}, u32[]{:S(2)}) collective-permute-start(f32[4,128,128]{2,1,0:T(8,128)S(1)} %maximum_add_fusion.6), channel_id=1, source_target_pairs={{0,16},{4,20},{8,24},{12,28},{16,32},{20,36},{24,40},{28,44},{32,4... | collective-permute-start | bytes 786440 | tf_op jit(solution)/shard_map/while/body/eval_jaxpr/ppermute | solution.py:9
  752.6 18.5 %collective-permute-start.3 = (f32[4,128,128]{2,1,0:T(8,128)}, f32[4,128,128]{2,1,0:T(8,128)S(1)}, u32[]{:S(2)}, u32[]{:S(2)}) collective-permute-start(f32[4,128,128]{2,1,0:T(8,128)} %maximum_add_fusion.7), channel_id=1, source_target_pairs={{0,16},{4,20},{8,24},{12,28},{16,32},{20,36},{24,40},{28,44},{32,4... | collective-permute-start | bytes 786440 | tf_op jit(solution)/shard_map/while/body/eval_jaxpr/ppermute | solution.py:9
  771.8 9.5 %collective-permute-start.12 = (f32[2,128,128]{2,1,0:T(8,128)S(1)}, f32[2,128,128]{2,1,0:T(8,128)S(1)}, u32[]{:S(2)}, u32[]{:S(2)}) collective-permute-start(f32[2,128,128]{2,1,0:T(8,128)S(1)} %slice.232), channel_id=1, source_target_pairs={{0,504},{4,508},{8,0},{12,4},{16,8},{20,12},{24,16},{28,20},{32,24... | collective-permute-start | bytes 393224 | tf_op jit(solution)/shard_map/ppermute | solution.py:9
  773.9 9.7 %collective-permute-start.16 = (f32[2,128,128]{2,1,0:T(8,128)S(1)}, f32[2,128,128]{2,1,0:T(8,128)S(1)}, u32[]{:S(2)}, u32[]{:S(2)}) collective-permute-start(f32[2,128,128]{2,1,0:T(8,128)S(1)} %slice.236), channel_id=1, source_target_pairs={{0,504},{4,508},{8,0},{12,4},{16,8},{20,12},{24,16},{28,20},{32,24... | collective-permute-start | bytes 393224 | tf_op jit(solution)/shard_map/ppermute | solution.py:9
  781.4 11.7 %collective-permute-start.13 = (f32[1,128,128]{2,1,0:T(8,128)S(1)}, f32[1,128,128]{2,1,0:T(8,128)S(1)}, u32[]{:S(2)}, u32[]{:S(2)}) collective-permute-start(f32[1,128,128]{2,1,0:T(8,128)S(1)} %slice.264), channel_id=1, source_target_pairs={{0,508},{4,0},{8,4},{12,8},{16,12},{20,16},{24,20},{28,24},{32,28}... | collective-permute-start | bytes 196616 | tf_op jit(solution)/shard_map/ppermute | solution.py:9
  783.6 11.4 %collective-permute-start.17 = (f32[1,128,128]{2,1,0:T(8,128)S(1)}, f32[1,128,128]{2,1,0:T(8,128)S(1)}, u32[]{:S(2)}, u32[]{:S(2)}) collective-permute-start(f32[1,128,128]{2,1,0:T(8,128)S(1)} %slice.266), channel_id=1, source_target_pairs={{0,508},{4,0},{8,4},{12,8},{16,12},{20,16},{24,20},{28,24},{32,28}... | collective-permute-start | bytes 196616 | tf_op jit(solution)/shard_map/ppermute | solution.py:9
  793.2 6.5 collective-permute-start.14
  795.1 11.4 %collective-permute-start.18 = (f32[128,128]{1,0:T(8,128)S(1)}, f32[128,128]{1,0:T(8,128)S(1)}, u32[]{:S(2)}, u32[]{:S(2)}) collective-permute-start(f32[128,128]{1,0:T(8,128)S(1)} %fusion.29), channel_id=1, source_target_pairs={{0,128},{4,132},{8,136},{12,140},{16,144},{20,148},{24,152},{28,15... | collective-permute-start | bytes 196616 | tf_op jit(solution)/shard_map/ppermute | solution.py:9
  799.7 8.8 collective-permute-start.15
  806.6 6.5 collective-permute-start.19
  (113 other events, 713.7 us)
where the time goes:
time: 914 us; the launch traced here: 909 us
  blocking collectives  565 us (62%)
  waiting for transfers between devices  150 us (16%)
  starting transfers between devices  112 us (12%)
  local copies, waits for them, and re-layouts  39.5 us (4%)
  matrix products  19.5 us (2%)
  other arithmetic  18.2 us (2%)
    all_gather x1, blocking collectives, per_device(): lax.all_gather(positions, 'blk', axis=0, tiled=True)  470 us
    ppermute x48, waiting for transfers between devices, shifted_2(): lax.ppermute(shard, axis, [(i, (i + by) % devices) for i in range(devices)])  150 us
    ppermute x48, starting transfers between devices, shifted_2(): lax.ppermute(shard, axis, [(i, (i + by) % devices) for i in range(devices)])  112 us
    psum x1, blocking collectives, per_device(): summed = lax.psum((grad_query, total_keys, total_values), 'rep')  95.8 us
    while x224, local copies, waits for them, and re-layouts  20.4 us
  transfers between devices with their start and end apart: 48, of which 31 were waited for; matrix products, arithmetic and copies ran while one was open for 7% of the time, Pallas kernels for 0%

commit v1 on v0

v1 whole, which is shorter than its diff:
```python
import math

import jax
import jax.numpy as jnp
from jax import lax
from jax.experimental import pallas as pl
from jax.experimental.pallas import tpu as pltpu
from jax.sharding import PartitionSpec as P

MESH = pl.DeviceIdType.MESH
BF = jnp.bfloat16
F32 = jnp.float32
HD = 128
SCALE = HD ** (-0.5)
LOG2E = math.log2(math.e)
BIG = 1e30
NEAR = (0, 1, 7, 2, 6, 3, 5, 4)
FAR = (4, 3, 5, 2, 6, 1, 7, 0)


def coords():
    b = lax.axis_index("blk")
    r = lax.axis_index("rep")
    x = b // 32
    y = b % 4
    z = (r // 2) * 8 + (b // 4) % 8
    return x, y, z, r % 2


def dev(x, y, z, c):
    xx = (x + 4) % 4
    yy = (y + 4) % 4
    zz = (z + 16) % 16
    return ((xx * 8 + zz % 8) * 4 + yy, (zz // 8) * 2 + c)


def zoff(s, c):
    if s < 4:
        return s
    if s > 4:
        return s - 8
    return 4 - 8 * c


def peers(x, y, z, c):
    out = [dev(x, y, z, 1 - c)]
    for d in (1, 2, 3):
        out.append(dev(x + d, y, z, c))
        out.append(dev(x, y + d, z, c))
    for o in (1, 2, 3, 4, -1, -2, -3, -4):
        out.append(dev(x, y, z + o, c))
    return out


def entry_barrier(x, y, z, c):
    barrier = pltpu.get_barrier_semaphore()
    group = peers(x, y, z, c)
    for d in group:
        pl.semaphore_signal(barrier, inc=1, device_id=d, device_id_type=MESH)
    pl.semaphore_wait(barrier, len(group))


def rcopy(src, dst, ssem, rsem, device):
    return pltpu.make_async_remote_copy(
        src_ref=src, dst_ref=dst, send_sem=ssem, recv_sem=rsem, device_id=device, device_id_type=MESH
    )


def gather_kernel(
    q_ref, k_ref, v_ref, o_ref, do_ref, lse_ref, pos_ref,
    qd_ref, sm_ref, kv_ref, kp_ref,
    zs, zr, ps, pr, ys, yr, bs, br, xs, xr, ms, mr, kys, kyr,
):
    x, y, z, c = coords()
    col = pl.multiple_of(c * 256, 256)
    qd_ref[0, 0] = q_ref[:, pl.ds(col, 256)]
    qd_ref[0, 1] = do_ref[:, pl.ds(col, 256)]
    kv_ref[0, 0, 0] = k_ref[...]
    kv_ref[1, 0, 0] = v_ref[...]
    kp_ref[0, 0] = pos_ref[...]
    entry_barrier(x, y, z, c)

    started = []

    def go(cp):
        cp.start()
        started.append(cp)
        return cp

    zc = {}
    for s in NEAR[1:]:
        o = zoff(s, c)
        zc[s] = go(rcopy(kv_ref.at[c, 0, 0], kv_ref.at[c, s, 0], zs.at[s], zr.at[s], dev(x, y, z - o, c)))
    pc = {}
    for s in NEAR[1:]:
        o = zoff(s, c)
        pc[s] = go(rcopy(kp_ref.at[0, 0], kp_ref.at[0, s], ps.at[s], pr.at[s], dev(x, y, z - o, c)))
    xc = {
        3: go(rcopy(qd_ref.at[0], qd_ref.at[3], xs.at[3], xr.at[3], dev(x + 1, y, z, c))),
        1: go(rcopy(qd_ref.at[0], qd_ref.at[1], xs.at[1], xr.at[1], dev(x - 1, y, z, c))),
    }
    rows = []
    for h in range(2):
        rows.append(lse_ref[pl.ds(2 * c + h, 1), :])
    for h in range(2):
        prod = do_ref[:, pl.ds(col + h * HD, HD)].astype(F32) * o_ref[:, pl.ds(col + h * HD, HD)].astype(F32)
        tot = jnp.sum(prod, axis=1, keepdims=True)
        rows.append(jnp.broadcast_to(tot, (HD, HD)).T[0:1, :])
    p = pos_ref[...]
    rows.append((p // 32768).astype(F32))
    rows.append((p % 32768).astype(F32))
    rows.append(jnp.zeros((2, HD), F32))
    sm_ref[0] = jnp.concatenate(rows, axis=0)
    mc = {}
    for d in (1, 2, 3):
        mc[d] = go(rcopy(sm_ref.at[0], sm_ref.at[d], ms.at[d], mr.at[d], dev(x - d, y, z, c)))

    yc, hc, bc = {}, {}, {}

    def stage_full(s):
        if s:
            zc[s].wait_recv()
            bc[s, 0] = go(
                rcopy(kv_ref.at[c, s, 0], kv_ref.at[c, s, 0], bs.at[s, 0], br.at[s, 0], dev(x, y, z, 1 - c))
            )
        yc[s, 3] = go(rcopy(kv_ref.at[c, s, 0], kv_ref.at[c, s, 3], ys.at[s, 0], yr.at[s, 0], dev(x, y + 1, z, c)))
        yc[s, 1] = go(rcopy(kv_ref.at[c, s, 0], kv_ref.at[c, s, 1], ys.at[s, 1], yr.at[s, 1], dev(x, y - 1, z, c)))

    def stage_half(s):
        top, bot = pl.ds(0, 64), pl.ds(64, 64)
        yc[s, 3].wait_recv()
        hc[s, 0] = go(
            rcopy(kv_ref.at[c, s, 3, top], kv_ref.at[c, s, 2, top], ys.at[s, 2], yr.at[s, 2], dev(x, y + 1, z, c))
        )
        yc[s, 1].wait_recv()
        hc[s, 1] = go(
            rcopy(kv_ref.at[c, s, 1, bot], kv_ref.at[c, s, 2, bot], ys.at[s, 3], yr.at[s, 3], dev(x, y - 1, z, c))
        )

    def stage_sib(s):
        hc[s, 0].wait_recv()
        hc[s, 1].wait_recv()
        rest = pl.ds(1, 3)
        bc[s, 1] = go(
            rcopy(kv_ref.at[c, s, rest], kv_ref.at[c, s, rest], bs.at[s, 1], br.at[s, 1], dev(x, y, z, 1 - c))
        )

    xh = {}
    for t in range(len(NEAR) + 2):
        if t < 8:
            stage_full(NEAR[t])
        if t == 2:
            top, bot = pl.ds(0, 64), pl.ds(64, 64)
            both = pl.ds(0, 2)
            xc[3].wait_recv()
            xh[0] = go(
                rcopy(qd_ref.at[3, both, top], qd_ref.at[2, both, top], xs.at[0], xr.at[0], dev(x + 1, y, z, c))
            )
            xc[1].wait_recv()
            xh[1] = go(
                rcopy(qd_ref.at[1, both, bot], qd_ref.at[2, both, bot], xs.at[2], xr.at[2], dev(x - 1, y, z, c))
            )
        if 1 <= t < 9:
            stage_half(NEAR[t - 1])
        if 2 <= t:
            stage_sib(NEAR[t - 2])
    for s in NEAR[1:]:
        pc[s].wait_recv()
    kc = {}
    for d in (1, 2, 3):
        kc[d] = go(rcopy(kp_ref.at[0], kp_ref.at[d], kys.at[d], kyr.at[d], dev(x, y - d, z, c)))
    xh[0].wait_recv()
    xh[1].wait_recv()
    for d in (1, 2, 3):
        mc[d].wait_recv()
        kc[d].wait_recv()
    for s in range(8):
        if s:
            rcopy(
                kv_ref.at[1 - c, s, 0], kv_ref.at[1 - c, s, 0], bs.at[s, 0], br.at[s, 0], dev(x, y, z, 1 - c)
            ).wait_recv()
        rest = pl.ds(1, 3)
        rcopy(
            kv_ref.at[1 - c, s, rest], kv_ref.at[1 - c, s, rest], bs.at[s, 1], br.at[s, 1], dev(x, y, z, 1 - c)
        ).wait_recv()
    for cp in started:
        cp.wait_send()


def nt(a, b):
    return lax.dot_general(a, b, (((1,), (1,)), ((), ())), preferred_element_type=F32)


def nn(a, b):
    return lax.dot_general(a, b, (((1,), (0,)), ((), ())), preferred_element_type=F32)


def compute_kernel(qd_ref, sm_ref, kv_ref, kp_ref, dkv_ref, dq_ref, qx, dx, rw, dqt):
    lane = lax.broadcasted_iota(jnp.int32, (8, HD), 1)
    for i in range(4):
        for h in range(2):
            for half in range(2):
                rows = pl.ds(64 * half, 64)
                cols = pl.ds(HD * h, HD)
                qx[half, pl.ds(i * HD + 64 * h, 64), :] = qd_ref[i, 0, rows, cols]
                dx[half, pl.ds(i * HD + 64 * h, 64), :] = qd_ref[i, 1, rows, cols]
        t = sm_ref[i]
        tr = pltpu.roll(t, 64, 1)
        sel = lane < 64
        qlo = t[4:5].astype(jnp.int32) * 32768 + t[5:6].astype(jnp.int32)
        qlo = jnp.broadcast_to(qlo[:, 0:1], (1, HD)).astype(jnp.int32)
        cs = pl.ds(i * HD, HD)
        lse = t[0:2] * LOG2E
        lser = tr[0:2] * LOG2E
        rw[0:1, cs] = jnp.where(sel[0:1], lse[0:1], lser[1:2])
        rw[1:2, cs] = jnp.where(sel[0:1], lser[0:1], lse[1:2])
        rw[2:3, cs] = jnp.where(sel[0:1], t[2:3], tr[3:4]) * SCALE
        rw[3:4, cs] = jnp.where(sel[0:1], tr[2:3], t[3:4]) * SCALE
        rw[4:5, cs] = jnp.where(qlo < 0, 0, qlo // 32768).astype(F32)
        rw[5:6, cs] = (qlo % 32768).astype(F32)
    dqt[...] = jnp.zeros_like(dqt)

    def chunk(s, diag):
        firsts = []
        for yb in range(4):
            firsts.append(kp_ref[yb, s][:, 0:1])
        for kh in range(2):
            rows = pl.ds(64 * kh, 64)
            kc = kv_ref[0, s, :, rows, :].reshape(256, HD)
            vc = kv_ref[1, s, :, rows, :].reshape(256, HD)
            kt = kc.T
            dk = jnp.zeros((256, HD), F32)
            dv = jnp.zeros((256, HD), F32)
            for half in ((0, 1) if kh == 0 else (1,)):
                for g in range(2):
                    ls = pl.ds(256 * g, 256)
                    lse = rw[half : half + 1, ls]
                    dlt = rw[2 + half : 3 + half, ls]
                    if kh != half:
                        le = jnp.broadcast_to(lse, (4, 256))
                    else:
                        qp = rw[4:5, ls].astype(jnp.int32) * 32768 + rw[5:6, ls].astype(jnp.int32)
                        parts = []
                        for yb in range(4):
                            kp = jnp.broadcast_to(firsts[yb], (1, 256))
                            seen = kp <= qp if kh == 0 else kp >= qp
                            parts.append(jnp.where(seen, lse, BIG))
                        le = jnp.concatenate(parts, axis=0)
                    qg = qx[half, ls, :]
                    dg = dx[half, ls, :]
                    sc = nt(kc, qg).reshape(4, 64, 256)
                    dp = nt(vc, dg)
                    t = sc * (SCALE * LOG2E) - le[:, None, :]
                    t = t.reshape(256, 256)
                    if diag and kh == half and g == 0:
                        ri = lax.broadcasted_iota(jnp.int32, (256, 256), 0)
                        li = lax.broadcasted_iota(jnp.int32, (256, 256), 1)
                        seen = (ri >= 64) | (li >= 128) | (ri <= li % 64)
                        t = jnp.where(seen, t, -BIG)
                    p = jnp.exp2(t)
                    ds = (p * (dp * SCALE - dlt)).astype(BF)
                    dv = dv + nn(p.astype(BF), dg)
                    dk = dk + nn(ds, qg)
                    dqt[half, :, ls] += nn(kt, ds)
            dkv_ref[0, s, :, rows, :] = dk.astype(BF).reshape(4, 64, HD)
            dkv_ref[1, s, :, rows, :] = dv.astype(BF).reshape(4, 64, HD)

    chunk(0, True)

    def body(s, carry):
        chunk(s, False)
        return carry

    lax.fori_loop(1, 8, body, 0)
    for i in range(4):
        for half in range(2):
            tile = dqt[half, :, pl.ds(i * HD, HD)].T.astype(BF)
            for h in range(2):
                dq_ref[i, pl.ds(64 * half, 64), pl.ds(HD * h, HD)] = tile[64 * h : 64 * h + 64]


def reduce_kernel(
    dkv_ref, dq_ref,
    gq_ref, gk_ref, gv_ref,
    sib, acc, fa, fb, ra, rb, zb, zin, fin, qin, qfin,
    bs, br, ys, yr, zs, zr, xs, xr, fs, fr,
):
    x, y, z, c = coords()
    entry_barrier(x, y, z, c)
    started = []

    def go(cp):
        cp.start()
        started.append(cp)
        return cp

    other = dev(x, y, z, 1 - c)
    top, bot = pl.ds(0, 64), pl.ds(64, 64)
    bc, qc, ac, rc, zc = {}, {}, {}, {}, {}
    for s in FAR:
        bc[s] = go(rcopy(dkv_ref.at[1 - c, s], sib.at[s], bs.at[s], br.at[s], other))
    for d in (2, 1, 3):
        qc[d] = go(rcopy(dq_ref.at[d], qin.at[d], xs.at[d], xr.at[d], dev(x + d, y, z, c)))

    def stage_a(s):
        bc[s].wait_recv()
        for d in (2, 1, 3):
            acc[s, d] = (dkv_ref[c, s, d].astype(F32) + sib[s, d].astype(F32)).astype(BF)
        ac[s, 0] = go(rcopy(acc.at[s, 2, top], fa.at[s], ys.at[s, 0], yr.at[s, 0], dev(x, y + 1, z, c)))
        ac[s, 1] = go(rcopy(acc.at[s, 2, bot], fb.at[s], ys.at[s, 1], yr.at[s, 1], dev(x, y - 1, z, c)))

    def stage_b(s):
        ac[s, 0].wait_recv()
        acc[s, 1, top] = (acc[s, 1, top].astype(F32) + fa[s].astype(F32)).astype(BF)
        rc[s, 0] = go(rcopy(acc.at[s, 1], ra.at[s], ys.at[s, 2], yr.at[s, 2], dev(x, y + 1, z, c)))
        ac[s, 1].wait_recv()
        acc[s, 3, bot] = (acc[s, 3, bot].astype(F32) + fb[s].astype(F32)).astype(BF)
        rc[s, 1] = go(rcopy(acc.at[s, 3], rb.at[s], ys.at[s, 3], yr.at[s, 3], dev(x, y - 1, z, c)))

    def stage_c(s):
        rc[s, 0].wait_recv()
        rc[s, 1].wait_recv()
        tot = dkv_ref[c, s, 0].astype(F32) + sib[s, 0].astype(F32) + ra[s].astype(F32) + rb[s].astype(F32)
        if s == 0:
            return tot
        zb[s] = tot.astype(BF)
        o = zoff(s, c)
        zc[s] = go(rcopy(zb.at[s], zin.at[s], zs.at[s], zr.at[s], dev(x, y, z + o, c)))
        return None

    tot = None
    for t in range(10):
        if t < 8:
            stage_a(FAR[t])
        if 1 <= t < 9:
            stage_b(FAR[t - 1])
        if 2 <= t:
            tot = stage_c(FAR[t - 2])
    for d in (1, 2, 3):
        qc[d].wait_recv()
    qsum = dq_ref[0].astype(F32)
    for d in (1, 2, 3):
        qsum = qsum + qin[d].astype(F32)
    qfin[0] = qsum.astype(BF)
    sq = go(rcopy(qfin.at[0], qfin.at[1], fs.at[0], fr.at[0], other))
    for s in range(1, 8):
        zc[s].wait_recv()
        tot = tot + zin[s].astype(F32)
    fin[0] = tot.astype(BF)
    sk = go(rcopy(fin.at[0], fin.at[1], fs.at[1], fr.at[1], other))
    low = c == 0
    sq.wait_recv()
    gq_ref[:, 0:256] = jnp.where(low, qfin[0], qfin[1])
    gq_ref[:, 256:512] = jnp.where(low, qfin[1], qfin[0])
    sk.wait_recv()
    gk_ref[...] = jnp.where(low, fin[0], fin[1])
    gv_ref[...] = jnp.where(low, fin[1], fin[0])
    for cp in started:
        cp.wait_send()


VM = pl.BlockSpec(memory_space=pltpu.VMEM)
DMA = pltpu.SemaphoreType.DMA


def per_device(queries, keys, values, output, grad_out, lse, positions):
    shapes = (
        jax.ShapeDtypeStruct((4, 2, 128, 256), BF),
        jax.ShapeDtypeStruct((4, 8, 128), F32),
        jax.ShapeDtypeStruct((2, 8, 4, 128, 128), BF),
        jax.ShapeDtypeStruct((4, 8, 1, 128), jnp.int32),
    )
    qd, sm, kv, kp = pl.pallas_call(
        gather_kernel,
        out_shape=shapes,
        in_specs=[VM] * 7,
        out_specs=(VM,) * 4,
        scratch_shapes=[
            DMA((8,)), DMA((8,)), DMA((8,)), DMA((8,)), DMA((8, 4)), DMA((8, 4)), DMA((8, 2)), DMA((8, 2)),
            DMA((4,)), DMA((4,)), DMA((4,)), DMA((4,)), DMA((4,)), DMA((4,)),
        ],
        compiler_params=pltpu.CompilerParams(collective_id=0, has_side_effects=True),
        name="gather",
    )(queries, keys, values, output, grad_out, lse, positions.reshape(1, 128))
    dkv, dq = pl.pallas_call(
        compute_kernel,
        out_shape=(
            jax.ShapeDtypeStruct((2, 8, 4, 128, 128), BF),
            jax.ShapeDtypeStruct((4, 128, 256), BF),
        ),
        in_specs=[VM] * 4,
        out_specs=(VM,) * 2,
        scratch_shapes=[
            pltpu.VMEM((2, 512, 128), BF),
            pltpu.VMEM((2, 512, 128), BF),
            pltpu.VMEM((8, 512), F32),
            pltpu.VMEM((2, 128, 512), F32),
        ],
        name="compute",
    )(qd, sm, kv, kp)
    return pl.pallas_call(
        reduce_kernel,
        out_shape=(
            jax.ShapeDtypeStruct((128, 512), BF),
            jax.ShapeDtypeStruct((128, 128), BF),
            jax.ShapeDtypeStruct((128, 128), BF),
        ),
        in_specs=[VM] * 2,
        out_specs=(VM,) * 3,
        scratch_shapes=[
            pltpu.VMEM((8, 4, 128, 128), BF),
            pltpu.VMEM((8, 4, 128, 128), BF),
            pltpu.VMEM((8, 64, 128), BF),
            pltpu.VMEM((8, 64, 128), BF),
            pltpu.VMEM((8, 128, 128), BF),
            pltpu.VMEM((8, 128, 128), BF),
            pltpu.VMEM((8, 128, 128), BF),
            pltpu.VMEM((8, 128, 128), BF),
            pltpu.VMEM((2, 128, 128), BF),
            pltpu.VMEM((4, 128, 256), BF),
            pltpu.VMEM((2, 128, 256), BF),
            DMA((8,)), DMA((8,)), DMA((8, 4)), DMA((8, 4)), DMA((8,)), DMA((8,)), DMA((4,)), DMA((4,)),
            DMA((2,)), DMA((2,)),
        ],
        compiler_params=pltpu.CompilerParams(collective_id=1, has_side_effects=True),
        name="reduce",
    )(dkv, dq)


def solution(mesh):
    placed = (
        P("blk", None),
        P("blk", None),
        P("blk", None),
        P("blk", None),
        P("blk", None),
        P(None, "blk"),
        P("blk"),
    )
    return jax.shard_map(
        per_device,
        mesh=mesh,
        in_specs=placed,
        out_specs=(P("blk", None), P("blk", None), P("blk", None)),
        check_vma=False,
    )
```

time: 914 us -> 98.4 us (0.11)
  blocking collectives: 565 us -> 0 us
  waiting for transfers between devices: 150 us -> 0 us
  starting transfers between devices: 112 us -> 0 us
  Pallas kernels: 0 us -> 93 us
  local copies, waits for them, and re-layouts: 39.5 us -> 4.32 us
  matrix products: 19.5 us -> 0 us
  other arithmetic: 18.2 us -> 0 us
    all_gather x1 -> x0, blocking collectives: 470 us -> none  [per_device(): lax.all_gather(positions, 'blk', axis=0, tiled=True)]
    ppermute x48 -> x0, waiting for transfers between devices: 150 us -> none  [shifted_2(): lax.ppermute(shard, axis, [(i, (i + by) % devices) for i in range(devices)])]
    ppermute x48 -> x0, starting transfers between devices: 112 us -> none  [shifted_2(): lax.ppermute(shard, axis, [(i, (i + by) % devices) for i in range(devices)])]
    psum x1 -> x0, blocking collectives: 95.8 us -> none  [per_device(): summed = lax.psum((grad_query, total_keys, total_values), 'rep')]
    pallas_call x0 -> x3, Pallas kernels: none -> 93 us  [the longest x1 41.8 us: per_device(): pl.pallas_call(gather_kernel, out_shape=shapes, in_specs=[VM] * 7, out_sp...]
    while x224 -> x0, local copies, waits for them, and re-layouts: 20.4 us -> none
    dot_general x45 -> x0, matrix products: 19.5 us -> none  [the longest x9 5.29 us: pair_terms(): jnp.einsum('pthd,pkd->phtk', query_part, key_part, preferred_element_type...]
  transfers between devices with their start and end apart: 48 -> 0, of which waited for: 31 -> 0; matrix products, arithmetic and copies ran while one was open for 7% -> 0% of each run, Pallas kernels for 0% -> 0%
where the time goes in v1:
time: 98.4 us; the launch traced here: 98 us
  Pallas kernels  93 us (95%)
  local copies, waits for them, and re-layouts  4.32 us (4%)
    pallas_call x1, Pallas kernels, per_device(): pl.pallas_call(gather_kernel, out_shape=shapes, in_specs=[VM] * 7, out_sp...  41.8 us
    pallas_call x1, Pallas kernels, per_device(): pl.pallas_call(reduce_kernel, out_shape=(jax.ShapeDtypeStruct((128, 512),...  35.2 us
    pallas_call x1, Pallas kernels, per_device(): pl.pallas_call(compute_kernel, out_shape=(jax.ShapeDtypeStruct((2, 8, 4,...  16 us
    unnamed x3, local copies, waits for them, and re-layouts  4.32 us

profile of v1, /device:TPU:1, one launch (start us, length us, event | category | flops | bytes accessed | tf_op | source)
XLA Modules:
  0.0 98.0 jit_solution(3928184218855433334)
XLA Ops:
  0.6 41.8 %gather.1 = (bf16[4,2,128,256]{3,2,1,0:T(8,128)(2,1)}, f32[4,8,128]{2,1,0:T(8,128)}, bf16[2,8,4,128,128]{4,3,2,1,0:T(8,128)(2,1)}, s32[4,8,1,128]{3,2,1,0:T(1,128)}) custom-call(bf16[128,512]{1,0:T(8,128)(2,1)} %q_ref.1, bf16[128,128]{1,0:T(8,128)(2,1)} %k_ref.1, bf16[128,128]{1,0:T(8,128)(2,1)} %v_ref.1, bf16[128,512]{1,0:T(8,128)(2,1)} %o_ref.1, ...), custom_call_target="tpu_custom_call" | custom-call | tf_op jit(solution)/shard_map/gather/pallas_call | solution.py:373
  42.5 16.0 %compute.1 = (bf16[2,8,4,128,128]{4,3,2,1,0:T(8,128)(2,1)}, bf16[4,128,256]{2,1,0:T(8,128)(2,1)}) custom-call(bf16[4,2,128,256]{3,2,1,0:T(8,128)(2,1)} %get-tuple-element.9.qd_ref, f32[4,8,128]{2,1,0:T(8,128)} %get-tuple-element.10.sm_ref, bf16[2,8,4,128,128]{4,3,2,1,0:T(8,128)(2,1)} %get-tuple-element.11.kv_ref, s32[4,8,1,128]{3,2,1,0:T(1,128)} %get-tuple-element.12.kp_ref), custom_call_target="tpu_custom_call" | custom-call | tf_op jit(solution)/shard_map/compute/pallas_call | solution.py:385
  58.4 35.2 %reduce.1 = (bf16[128,512]{1,0:T(8,128)(2,1)}, bf16[128,128]{1,0:T(8,128)(2,1)}, bf16[128,128]{1,0:T(8,128)(2,1)}) custom-call(bf16[2,8,4,128,128]{4,3,2,1,0:T(8,128)(2,1)} %get-tuple-element.13.dkv_ref, bf16[4,128,256]{2,1,0:T(8,128)(2,1)} %get-tuple-element.14.dq_ref), custom_call_target="tpu_custom_call" | custom-call | tf_op jit(solution)/shard_map/reduce/pallas_call | solution.py:401
  93.7 1.6 %copy.13 = bf16[128,512]{1,0:T(8,128)(2,1)} copy(bf16[128,512]{1,0:T(8,128)(2,1)} %get-tuple-element.18) | data formatting | bytes 262144
  95.2 1.4 %copy.14 = bf16[128,128]{1,0:T(8,128)(2,1)} copy(bf16[128,128]{1,0:T(8,128)(2,1)} %get-tuple-element.19) | data formatting | bytes 65536
  96.6 1.4 %copy.15 = bf16[128,128]{1,0:T(8,128)(2,1)} copy(bf16[128,128]{1,0:T(8,128)(2,1)} %get-tuple-element.20) | data formatting | bytes 65536

commit v2 on v1

v2 whole, which is shorter than its diff:
```python
import math

import jax
import jax.numpy as jnp
from jax import lax
from jax.experimental import pallas as pl
from jax.experimental.pallas import tpu as pltpu
from jax.sharding import PartitionSpec as P

MESH = pl.DeviceIdType.MESH
BF = jnp.bfloat16
F32 = jnp.float32
HD = 128
SCALE = HD ** (-0.5)
LOG2E = math.log2(math.e)
BIG = 1e30
NEAR = (0, 1, 7, 2, 6, 3, 5, 4)
FAR = (4, 3, 5, 2, 6, 1, 7, 0)


def coords():
    b = lax.axis_index("blk")
    r = lax.axis_index("rep")
    x = b // 32
    y = b % 4
    z = (r // 2) * 8 + (b // 4) % 8
    return x, y, z, r % 2


def dev(x, y, z, c):
    xx = (x + 4) % 4
    yy = (y + 4) % 4
    zz = (z + 16) % 16
    return ((xx * 8 + zz % 8) * 4 + yy, (zz // 8) * 2 + c)


def zoff(s, c):
    return (s + 3 + c) % 8 - 3 - c


def entry_barrier(x, y, z, c):
    group = [dev(x, y, z, 1 - c)]
    for d in (1, 2, 3):
        group.append(dev(x + d, y, z, c))
        group.append(dev(x, y + d, z, c))
    for o in (1, 2, 3, 4, -1, -2, -3, -4):
        group.append(dev(x, y, z + o, c))
    barrier = pltpu.get_barrier_semaphore()
    for d in group:
        pl.semaphore_signal(barrier, inc=1, device_id=d, device_id_type=MESH)
    return barrier, len(group)


def rcopy(src, dst, ssem, rsem, device):
    return pltpu.make_async_remote_copy(
        src_ref=src, dst_ref=dst, send_sem=ssem, recv_sem=rsem, device_id=device, device_id_type=MESH
    )


def nt(a, b):
    return lax.dot_general(a, b, (((1,), (1,)), ((), ())), preferred_element_type=F32)


def nn(a, b):
    return lax.dot_general(a, b, (((1,), (0,)), ((), ())), preferred_element_type=F32)


def prepare_rows(sm_ref, rw):
    sel = lax.broadcasted_iota(jnp.int32, (1, HD), 1) < 64
    for i in range(4):
        t = sm_ref[i]
        tr = pltpu.roll(t, 64, 1)
        cs = pl.ds(i * HD, HD)
        lse = t[0:2] * LOG2E
        lser = tr[0:2] * LOG2E
        rw[0:1, cs] = jnp.where(sel, lse[0:1], lser[1:2])
        rw[1:2, cs] = jnp.where(sel, lser[0:1], lse[1:2])
        rw[2:3, cs] = jnp.where(sel, t[2:3], tr[3:4]) * SCALE
        rw[3:4, cs] = jnp.where(sel, tr[2:3], t[3:4]) * SCALE
        rw[4:6, cs] = jnp.broadcast_to(t[4:6, 0:1], (2, HD))


def key_half(s, kh, qx, rw, kv_ref, kp_ref, dkv, dqt):
    rows = pl.ds(64 * kh, 64)
    kc = kv_ref[0, s, :, rows, :].reshape(256, HD)
    vc = kv_ref[1, s, :, rows, :].reshape(256, HD)
    kt = kc.T
    dk = jnp.zeros((256, HD), F32)
    dv = jnp.zeros((256, HD), F32)
    for half in ((0, 1) if kh == 0 else (1,)):
        for g in range(2):
            ls = pl.ds(256 * g, 256)
            lse = rw[half : half + 1, ls]
            dlt = rw[2 + half : 3 + half, ls]
            if kh != half:
                le = jnp.broadcast_to(lse, (4, 256))
            else:
                qp = rw[4:5, ls].astype(jnp.int32) * 32768 + rw[5:6, ls].astype(jnp.int32)
                parts = []
                for yb in range(4):
                    kp = jnp.broadcast_to(kp_ref[yb, s][:, 0:1], (1, 256))
                    seen = kp <= qp if kh == 0 else kp >= qp
                    parts.append(jnp.where(seen, lse, BIG))
                le = jnp.concatenate(parts, axis=0)
            qg = qx[0, half, 2 * g : 2 * g + 2].reshape(256, HD)
            dg = qx[1, half, 2 * g : 2 * g + 2].reshape(256, HD)
            sc = nt(kc, qg).reshape(4, 64, 256)
            dp = nt(vc, dg)
            t = (sc * (SCALE * LOG2E) - le[:, None, :]).reshape(256, 256)
            if kh == half and g == 0:
                ri = lax.broadcasted_iota(jnp.int32, (64, HD), 0)
                li = lax.broadcasted_iota(jnp.int32, (64, HD), 1)
                own = jnp.where(ri <= li % 64 + 64 * s, t[:64, :HD], -BIG)
                t = jnp.concatenate([jnp.concatenate([own, t[:64, HD:]], axis=1), t[64:]], axis=0)
            p = jnp.exp2(t)
            ds = (p * (dp * SCALE - dlt)).astype(BF)
            dv = dv + nn(p.astype(BF), dg)
            dk = dk + nn(ds, qg)
            dqt[half, :, ls] += nn(kt, ds)
    dkv[s, 0, :, rows, :] = dk.reshape(4, 64, HD)
    dkv[s, 1, :, rows, :] = dv.reshape(4, 64, HD)


def fused_kernel(
    q_ref, k_ref, v_ref, o_ref, do_ref, lse_ref, pos_ref,
    gq_ref, gk_ref, gv_ref,
    qx, sm, kv, kp, rw, dqt, dkv, so, sib, acc, fa, fb, ra, rb, rc, zb, zin, tot0, dqs, qin, fin, qfin,
    zs, zr, pzs, pzr, ys, yr, kys, kyr, bs, br, xs, xr, ms, mr,
    rbs, rbr, rys, ryr, rzs, rzr, rxs, rxr, fs, fr,
):
    x, y, z, c = coords()
    barrier, count = entry_barrier(x, y, z, c)
    other = dev(x, y, z, 1 - c)
    up, down = dev(x, y + 1, z, c), dev(x, y - 1, z, c)
    right, left = dev(x + 1, y, z, c), dev(x - 1, y, z, c)
    top, bot = pl.ds(0, 64), pl.ds(64, 64)
    rest = pl.ds(1, 3)
    col = pl.multiple_of(c * 256, 256)

    for h in range(2):
        for half in range(2):
            for n, ref in ((0, q_ref), (1, do_ref)):
                qx[n, half, 0, pl.ds(64 * h, 64), :] = ref[pl.ds(64 * half, 64), pl.ds(col + HD * h, HD)]
    kv[0, 0, 0] = k_ref[...]
    kv[1, 0, 0] = v_ref[...]
    kp[0, 0] = pos_ref[...]
    rows = []
    for h in range(2):
        rows.append(lse_ref[pl.ds(2 * c + h, 1), :])
    for h in range(2):
        prod = do_ref[:, pl.ds(col + h * HD, HD)].astype(F32) * o_ref[:, pl.ds(col + h * HD, HD)].astype(F32)
        total = jnp.sum(prod, axis=1, keepdims=True)
        rows.append(jnp.broadcast_to(total, (HD, HD)).T[0:1, :])
    p = pos_ref[...]
    rows.append((p // 32768).astype(F32))
    rows.append((p % 32768).astype(F32))
    rows.append(jnp.zeros((2, HD), F32))
    sm[0] = jnp.concatenate(rows, axis=0)
    pl.semaphore_wait(barrier, count)

    def z_copy(s):
        return rcopy(kv.at[c, 0, 0], kv.at[c, s, 0], zs.at[s], zr.at[s], dev(x, y, z - zoff(s, c), c))

    def pz_copy(s):
        return rcopy(kp.at[0, 0], kp.at[0, s], pzs.at[s], pzr.at[s], dev(x, y, z - zoff(s, c), c))

    def ky_copy(s, d):
        return rcopy(kp.at[0, s], kp.at[d, s], kys.at[s, d], kyr.at[s, d], dev(x, y - d, z, c))

    def full_up(s):
        return rcopy(kv.at[c, s, 0], kv.at[c, s, 3], ys.at[s, 0], yr.at[s, 0], up)

    def full_down(s):
        return rcopy(kv.at[c, s, 0], kv.at[c, s, 1], ys.at[s, 1], yr.at[s, 1], down)

    def half_up(s):
        return rcopy(kv.at[c, s, 3, top], kv.at[c, s, 2, top], ys.at[s, 2], yr.at[s, 2], up)

    def half_down(s):
        return rcopy(kv.at[c, s, 1, bot], kv.at[c, s, 2, bot], ys.at[s, 3], yr.at[s, 3], down)

    opp0 = rcopy(kv.at[c, 0, 0], kv.at[c, 0, 2], ys.at[0, 2], yr.at[0, 2], dev(x, y + 2, z, c))

    def sib_own(s, kind):
        return rcopy(kv.at[kind, s, 0], kv.at[kind, s, 0], bs.at[s, 0], br.at[s, 0], other)

    def sib_rest(s, kind):
        return rcopy(kv.at[kind, s, rest], kv.at[kind, s, rest], bs.at[s, 1], br.at[s, 1], other)

    def x_copy(n):
        src, dst, half, to = (
            (0, 3, 0, right), (0, 3, 1, right), (0, 1, 1, left), (0, 1, 0, left), (3, 2, 0, right), (1, 2, 1, left)
        )[n]
        return rcopy(qx.at[:, half, src], qx.at[:, half, dst], xs.at[n], xr.at[n], to)

    def m_copy(d):
        return rcopy(sm.at[0], sm.at[d], ms.at[d], mr.at[d], dev(x - d, y, z, c))

    def stage_full(s):
        z_copy(s).wait_recv()
        full_up(s).start()
        full_down(s).start()
        sib_own(s, c).start()
        pz_copy(s).wait_recv()
        for d in (1, 2, 3):
            ky_copy(s, d).start()

    def stage_half(s):
        full_up(s).wait_recv()
        half_up(s).start()
        full_down(s).wait_recv()
        half_down(s).start()

    def stage_sib(s):
        half_up(s).wait_recv()
        half_down(s).wait_recv()
        sib_rest(s, c).start()

    def rs_copy(s):
        return rcopy(so.at[s], sib.at[s], rbs.at[s], rbr.at[s], other)

    def ra_top(s):
        return rcopy(acc.at[s, 2, top], fa.at[s], rys.at[s, 0], ryr.at[s, 0], up)

    def ra_bot(s):
        return rcopy(acc.at[s, 2, bot], fb.at[s], rys.at[s, 1], ryr.at[s, 1], down)

    def rb_up(s):
        return rcopy(acc.at[s, 1], ra.at[s], rys.at[s, 2], ryr.at[s, 2], up)

    def rb_down(s):
        return rcopy(acc.at[s, 3], rb.at[s], rys.at[s, 3], ryr.at[s, 3], down)

    opp7 = rcopy(acc.at[7, 2], rc, rys.at[7, 0], ryr.at[7, 0], dev(x, y + 2, z, c))

    def rz_copy(s):
        return rcopy(zb.at[s], zin.at[s], rzs.at[s], rzr.at[s], dev(x, y, z + zoff(s, c), c))

    def rx_copy(d):
        return rcopy(dqs.at[d], qin.at[d], rxs.at[d], rxr.at[d], dev(x + d, y, z, c))

    def presum(s):
        rs_copy(s).wait_recv()
        for d in (2, 1, 3):
            acc[s, d] = (dkv[s, c, d] + sib[s, d].astype(F32)).astype(BF)

    def stage_a(s):
        presum(s)
        ra_top(s).start()
        ra_bot(s).start()

    def stage_b(s):
        ra_top(s).wait_recv()
        acc[s, 1, top] = (acc[s, 1, top].astype(F32) + fa[s].astype(F32)).astype(BF)
        rb_up(s).start()
        ra_bot(s).wait_recv()
        acc[s, 3, bot] = (acc[s, 3, bot].astype(F32) + fb[s].astype(F32)).astype(BF)
        rb_down(s).start()

    def own_sum(s):
        rb_up(s).wait_recv()
        rb_down(s).wait_recv()
        return dkv[s, c, 0] + sib[s, 0].astype(F32) + ra[s].astype(F32) + rb[s].astype(F32)

    full_up(0).start()
    full_down(0).start()
    opp0.start()
    for s in range(1, 8):
        z_copy(s).start()
    for n in range(4):
        x_copy(n).start()
    for d in (1, 2, 3):
        m_copy(d).start()
        ky_copy(0, d).start()
    for s in range(1, 8):
        pz_copy(s).start()
    dqt[...] = jnp.zeros_like(dqt)
    stage_full(1)
    full_up(0).wait_recv()
    full_down(0).wait_recv()
    opp0.wait_recv()
    sib_rest(0, c).start()
    x_copy(0).wait_recv()
    x_copy(4).start()
    x_copy(2).wait_recv()
    x_copy(5).start()
    stage_full(2)
    stage_half(1)
    stage_full(3)
    for d in (1, 2, 3):
        m_copy(d).wait_recv()
    prepare_rows(sm, rw)
    for n in (1, 3, 4, 5):
        x_copy(n).wait_recv()

    def slot(s, carry):
        @pl.when(s < 4)
        def _():
            stage_full(s + 4)

        @pl.when(s < 6)
        def _():
            stage_half(s + 2)

        @pl.when(s < 7)
        def _():
            stage_sib(s + 1)

        @pl.when(s > 0)
        def _():
            sib_own(s, 1 - c).wait_recv()

        sib_rest(s, 1 - c).wait_recv()
        for d in (1, 2, 3):
            ky_copy(s, d).wait_recv()
        key_half(s, 0, qx, rw, kv, kp, dkv, dqt)

        @pl.when(s > 0)
        def _():
            stage_a(s - 1)

        @pl.when(s > 1)
        def _():
            stage_b(s - 2)

        @pl.when(s == 3)
        def _():
            tot0[...] = own_sum(0)

        @pl.when(s > 3)
        def _():
            zb[s - 3] = own_sum(s - 3).astype(BF)
            rz_copy(s - 3).start()

        key_half(s, 1, qx, rw, kv, kp, dkv, dqt)
        so[s] = dkv[s, 1 - c].astype(BF)
        rs_copy(s).start()
        return carry

    lax.fori_loop(0, 8, slot, 0)
    for i in (2, 1, 3, 0):
        for half in range(2):
            tile = dqt[half, :, pl.ds(i * HD, HD)].T.astype(BF)
            for h in range(2):
                dqs[i, pl.ds(64 * half, 64), pl.ds(HD * h, HD)] = tile[64 * h : 64 * h + 64]
        if i:
            rx_copy(i).start()
    presum(7)
    opp7.start()
    rb_up(7).start()
    rb_down(7).start()
    stage_b(6)

    def to_owner(s):
        zb[s] = own_sum(s).astype(BF)
        rz_copy(s).start()

    to_owner(5)
    opp7.wait_recv()
    zb[7] = (own_sum(7) + rc[...].astype(F32)).astype(BF)
    rz_copy(7).start()
    to_owner(6)
    qsum = dqs[0].astype(F32)
    for d in (1, 3, 2):
        rx_copy(d).wait_recv()
        qsum = qsum + qin[d].astype(F32)
    qfin[0] = qsum.astype(BF)
    sq = rcopy(qfin.at[0], qfin.at[1], fs.at[0], fr.at[0], other)
    sq.start()
    tot = tot0[...]
    for s in range(1, 8):
        rz_copy(s).wait_recv()
        tot = tot + zin[s].astype(F32)
    fin[0] = tot.astype(BF)
    sk = rcopy(fin.at[0], fin.at[1], fs.at[1], fr.at[1], other)
    sk.start()
    low = c == 0
    sq.wait_recv()
    gq_ref[:, 0:256] = jnp.where(low, qfin[0], qfin[1])
    gq_ref[:, 256:512] = jnp.where(low, qfin[1], qfin[0])
    for n in range(6):
        x_copy(n).wait_send()
    for d in (1, 2, 3):
        m_copy(d).wait_send()
        rx_copy(d).wait_send()
    full_up(0).wait_send()
    full_down(0).wait_send()
    opp0.wait_send()
    sib_rest(0, c).wait_send()
    rs_copy(0).wait_send()
    for d in (1, 2, 3):
        ky_copy(0, d).wait_send()
    opp7.wait_send()
    ra_top(0).wait_send()
    ra_bot(0).wait_send()
    rb_up(0).wait_send()
    rb_down(0).wait_send()

    def drain(s, carry):
        z_copy(s).wait_send()
        pz_copy(s).wait_send()
        full_up(s).wait_send()
        full_down(s).wait_send()
        half_up(s).wait_send()
        half_down(s).wait_send()
        sib_own(s, c).wait_send()
        sib_rest(s, c).wait_send()
        for d in (1, 2, 3):
            ky_copy(s, d).wait_send()
        rs_copy(s).wait_send()
        rb_up(s).wait_send()
        rb_down(s).wait_send()
        rz_copy(s).wait_send()

        @pl.when(s < 7)
        def _():
            ra_top(s).wait_send()
            ra_bot(s).wait_send()

        return carry

    lax.fori_loop(1, 8, drain, 0)
    sq.wait_send()
    sk.wait()
    gk_ref[...] = jnp.where(low, fin[0], fin[1])
    gv_ref[...] = jnp.where(low, fin[1], fin[0])


VM = pl.BlockSpec(memory_space=pltpu.VMEM)
DMA = pltpu.SemaphoreType.DMA


def per_device(queries, keys, values, output, grad_out, lse, positions):
    return pl.pallas_call(
        fused_kernel,
        out_shape=(
            jax.ShapeDtypeStruct((128, 512), BF),
            jax.ShapeDtypeStruct((128, 128), BF),
            jax.ShapeDtypeStruct((128, 128), BF),
        ),
        in_specs=[VM] * 7,
        out_specs=(VM,) * 3,
        scratch_shapes=[
            pltpu.VMEM((2, 2, 4, 128, 128), BF),
            pltpu.VMEM((4, 8, 128), F32),
            pltpu.VMEM((2, 8, 4, 128, 128), BF),
            pltpu.VMEM((4, 8, 1, 128), jnp.int32),
            pltpu.VMEM((8, 512), F32),
            pltpu.VMEM((2, 128, 512), F32),
            pltpu.VMEM((8, 2, 4, 128, 128), F32),
            pltpu.VMEM((8, 4, 128, 128), BF),
            pltpu.VMEM((8, 4, 128, 128), BF),
            pltpu.VMEM((8, 4, 128, 128), BF),
            pltpu.VMEM((8, 64, 128), BF),
            pltpu.VMEM((8, 64, 128), BF),
            pltpu.VMEM((8, 128, 128), BF),
            pltpu.VMEM((8, 128, 128), BF),
            pltpu.VMEM((128, 128), BF),
            pltpu.VMEM((8, 128, 128), BF),
            pltpu.VMEM((8, 128, 128), BF),
            pltpu.VMEM((128, 128), F32),
            pltpu.VMEM((4, 128, 256), BF),
            pltpu.VMEM((4, 128, 256), BF),
            pltpu.VMEM((2, 128, 128), BF),
            pltpu.VMEM((2, 128, 256), BF),
            DMA((8,)), DMA((8,)), DMA((8,)), DMA((8,)), DMA((8, 4)), DMA((8, 4)), DMA((8, 4)), DMA((8, 4)),
            DMA((8, 2)), DMA((8, 2)), DMA((6,)), DMA((6,)), DMA((4,)), DMA((4,)),
            DMA((8,)), DMA((8,)), DMA((8, 4)), DMA((8, 4)), DMA((8,)), DMA((8,)), DMA((4,)), DMA((4,)),
            DMA((2,)), DMA((2,)),
        ],
        compiler_params=pltpu.CompilerParams(collective_id=0, has_side_effects=True),
        name="attention_grad",
    )(queries, keys, values, output, grad_out, lse, positions.reshape(1, 128))


def solution(mesh):
    placed = (
        P("blk", None),
        P("blk", None),
        P("blk", None),
        P("blk", None),
        P("blk", None),
        P(None, "blk"),
        P("blk"),
    )
    return jax.shard_map(
        per_device,
        mesh=mesh,
        in_specs=placed,
        out_specs=(P("blk", None), P("blk", None), P("blk", None)),
        check_vma=False,
    )
```

time: 98.4 us -> 67.3 us (0.68)
  Pallas kernels: 93 us -> 63 us
  local copies, waits for them, and re-layouts: 4.32 us -> 2.96 us
    pallas_call x3 -> x1, Pallas kernels: 93 us -> 63 us  [per_device(): pl.pallas_call(fused_kernel, out_shape=(jax.ShapeDtypeStruct((128, 512),...]
    unnamed x3 -> x7, local copies, waits for them, and re-layouts: 4.32 us -> 2.96 us
where the time goes in v2:
time: 67.3 us; the launch traced here: 66.7 us
  Pallas kernels  63 us (94%)
  local copies, waits for them, and re-layouts  2.96 us (4%)
    pallas_call x1, Pallas kernels, per_device(): pl.pallas_call(fused_kernel, out_shape=(jax.ShapeDtypeStruct((128, 512),...  63 us
    unnamed x7, local copies, waits for them, and re-layouts  2.96 us

profile of v2, /device:TPU:1, one launch (start us, length us, event | category | flops | bytes accessed | tf_op | source)
XLA Modules:
  0.0 66.7 jit_solution(11751556028110488893)
XLA Ops:
  0.6 63.0 %attention_grad.1 = (bf16[128,512]{1,0:T(8,128)(2,1)}, bf16[128,128]{1,0:T(8,128)(2,1)}, bf16[128,128]{1,0:T(8,128)(2,1)}) custom-call(bf16[128,512]{1,0:T(8,128)(2,1)} %q_ref.1, bf16[128,128]{1,0:T(8,128)(2,1)} %k_ref.1, bf16[128,128]{1,0:T(8,128)(2,1)} %v_ref.1, bf16[128,512]{1,0:T(8,128)(2,1)} %o_ref.1, bf16[128,512]{1,0:T(8,128)(2,1)} %do_ref.1, ...), custom_call_target="tpu_custom_call" | custom-call | tf_op jit(solution)/shard_map/attention_grad/pallas_call | solution.py:434
  63.7 0.0 copy-start.1
  63.7 1.6 %copy.13 = bf16[128,512]{1,0:T(8,128)(2,1)} copy(bf16[128,512]{1,0:T(8,128)(2,1)} %get-tuple-element.6) | data formatting | bytes 262144
  65.3 0.0 copy-done.1
  65.3 0.0 copy-start
  65.3 0.6 copy.14
  65.9 0.2 copy-done
  66.0 0.6 copy.15
Async XLA Ops:
  63.7 1.6 %copy-start.1 = (bf16[128,128]{1,0:T(8,128)(2,1)S(1)}, bf16[128,128]{1,0:T(8,128)(2,1)}, u32[]{:S(2)}) copy-start(bf16[128,128]{1,0:T(8,128)(2,1)} %get-tuple-element.7) | copy-start | bytes 98308
  65.3 0.8 %copy-start = (bf16[128,128]{1,0:T(8,128)(2,1)S(1)}, bf16[128,128]{1,0:T(8,128)(2,1)}, u32[]{:S(2)}) copy-start(bf16[128,128]{1,0:T(8,128)(2,1)} %get-tuple-element.8) | copy-start | bytes 98308

commit v3 on v2

--- a/solution.py
+++ b/solution.py
@@ -14,8 +14,7 @@
 SCALE = HD ** (-0.5)
 LOG2E = math.log2(math.e)
 BIG = 1e30
-NEAR = (0, 1, 7, 2, 6, 3, 5, 4)
-FAR = (4, 3, 5, 2, 6, 1, 7, 0)
+DIRECT = 5
 
 
 def coords():
@@ -125,8 +124,7 @@
     q_ref, k_ref, v_ref, o_ref, do_ref, lse_ref, pos_ref,
     gq_ref, gk_ref, gv_ref,
     qx, sm, kv, kp, rw, dqt, dkv, so, sib, acc, fa, fb, ra, rb, rc, zb, zin, tot0, dqs, qin, fin, qfin,
-    zs, zr, pzs, pzr, ys, yr, kys, kyr, bs, br, xs, xr, ms, mr,
-    rbs, rbr, rys, ryr, rzs, rzr, rxs, rxr, fs, fr,
+    ss, zr, yr, br, xr, cr, rbr, ryr,
 ):
     x, y, z, c = coords()
     barrier, count = entry_barrier(x, y, z, c)
@@ -159,51 +157,48 @@
     pl.semaphore_wait(barrier, count)
 
     def z_copy(s):
-        return rcopy(kv.at[c, 0, 0], kv.at[c, s, 0], zs.at[s], zr.at[s], dev(x, y, z - zoff(s, c), c))
+        return rcopy(kv.at[c, 0, 0], kv.at[c, s, 0], ss.at[0], zr.at[s], dev(x, y, z - zoff(s, c), c))
 
     def pz_copy(s):
-        return rcopy(kp.at[0, 0], kp.at[0, s], pzs.at[s], pzr.at[s], dev(x, y, z - zoff(s, c), c))
-
-    def ky_copy(s, d):
-        return rcopy(kp.at[0, s], kp.at[d, s], kys.at[s, d], kyr.at[s, d], dev(x, y - d, z, c))
+        return rcopy(kp.at[0, 0], kp.at[0, s], ss.at[1], cr.at[0], dev(x, y, z - zoff(s, c), c))
+
+    def ky_copy(d):
+        return rcopy(kp.at[0], kp.at[d], ss.at[2], cr.at[1], dev(x, y - d, z, c))
 
     def full_up(s):
-        return rcopy(kv.at[c, s, 0], kv.at[c, s, 3], ys.at[s, 0], yr.at[s, 0], up)
+        return rcopy(kv.at[c, s, 0], kv.at[c, s, 3], ss.at[3], yr.at[s, 0], up)
 
     def full_down(s):
-        return rcopy(kv.at[c, s, 0], kv.at[c, s, 1], ys.at[s, 1], yr.at[s, 1], down)
+        return rcopy(kv.at[c, s, 0], kv.at[c, s, 1], ss.at[4], yr.at[s, 1], down)
 
     def half_up(s):
-        return rcopy(kv.at[c, s, 3, top], kv.at[c, s, 2, top], ys.at[s, 2], yr.at[s, 2], up)
+        return rcopy(kv.at[c, s, 3, top], kv.at[c, s, 2, top], ss.at[5], yr.at[s, 2], up)
 
     def half_down(s):
-        return rcopy(kv.at[c, s, 1, bot], kv.at[c, s, 2, bot], ys.at[s, 3], yr.at[s, 3], down)
-
-    opp0 = rcopy(kv.at[c, 0, 0], kv.at[c, 0, 2], ys.at[0, 2], yr.at[0, 2], dev(x, y + 2, z, c))
-
-    def sib_own(s, kind):
-        return rcopy(kv.at[kind, s, 0], kv.at[kind, s, 0], bs.at[s, 0], br.at[s, 0], other)
-
-    def sib_rest(s, kind):
-        return rcopy(kv.at[kind, s, rest], kv.at[kind, s, rest], bs.at[s, 1], br.at[s, 1], other)
+        return rcopy(kv.at[c, s, 1, bot], kv.at[c, s, 2, bot], ss.at[6], yr.at[s, 3], down)
+
+    opp0 = rcopy(kv.at[c, 0, 0], kv.at[c, 0, 2], ss.at[7], yr.at[0, 2], dev(x, y + 2, z, c))
+
+    def sib_own(s):
+        return rcopy(kv.at[c, s, 0], kv.at[c, s, 0], ss.at[8], br.at[s], other)
+
+    def sib_rest(s):
+        return rcopy(kv.at[c, s, rest], kv.at[c, s, rest], ss.at[9], br.at[s], other)
 
     def x_copy(n):
         src, dst, half, to = (
             (0, 3, 0, right), (0, 3, 1, right), (0, 1, 1, left), (0, 1, 0, left), (3, 2, 0, right), (1, 2, 1, left)
         )[n]
-        return rcopy(qx.at[:, half, src], qx.at[:, half, dst], xs.at[n], xr.at[n], to)
+        return rcopy(qx.at[:, half, src], qx.at[:, half, dst], ss.at[10 + n], xr.at[n], to)
 
     def m_copy(d):
-        return rcopy(sm.at[0], sm.at[d], ms.at[d], mr.at[d], dev(x - d, y, z, c))
+        return rcopy(sm.at[0], sm.at[d], ss.at[16], cr.at[2], dev(x - d, y, z, c))
 
     def stage_full(s):
         z_copy(s).wait_recv()
         full_up(s).start()
         full_down(s).start()
-        sib_own(s, c).start()
-        pz_copy(s).wait_recv()
-        for d in (1, 2, 3):
-            ky_copy(s, d).start()
+        sib_own(s).start()
 
     def stage_half(s):
         full_up(s).wait_recv()
@@ -214,30 +209,43 @@
     def stage_sib(s):
         half_up(s).wait_recv()
         half_down(s).wait_recv()
-        sib_rest(s, c).start()
+        sib_rest(s).start()
+
+    def all_of(ref, sem):
+        return pltpu.make_async_copy(ref, ref, sem)
 
     def rs_copy(s):
-        return rcopy(so.at[s], sib.at[s], rbs.at[s], rbr.at[s], other)
+        return rcopy(so.at[s], sib.at[s], ss.at[17], rbr.at[s], other)
 
     def ra_top(s):
-        return rcopy(acc.at[s, 2, top], fa.at[s], rys.at[s, 0], ryr.at[s, 0], up)
+        return rcopy(acc.at[s, 2, top], fa.at[s], ss.at[18], ryr.at[s, 0], up)
 
     def ra_bot(s):
-        return rcopy(acc.at[s, 2, bot], fb.at[s], rys.at[s, 1], ryr.at[s, 1], down)
+        return rcopy(acc.at[s, 2, bot], fb.at[s], ss.at[19], ryr.at[s, 1], down)
 
     def rb_up(s):
-        return rcopy(acc.at[s, 1], ra.at[s], rys.at[s, 2], ryr.at[s, 2], up)
+        return rcopy(acc.at[s, 1], ra.at[s], ss.at[20], ryr.at[s, 2], up)
 
     def rb_down(s):
-        return rcopy(acc.at[s, 3], rb.at[s], rys.at[s, 3], ryr.at[s, 3], down)
-
-    opp7 = rcopy(acc.at[7, 2], rc, rys.at[7, 0], ryr.at[7, 0], dev(x, y + 2, z, c))
+        return rcopy(acc.at[s, 3], rb.at[s], ss.at[21], ryr.at[s, 3], down)
+
+    def ro_copy(s):
+        return rcopy(acc.at[s, 2], rc.at[s - DIRECT], ss.at[22], ryr.at[s, 0], dev(x, y + 2, z, c))
 
     def rz_copy(s):
-        return rcopy(zb.at[s], zin.at[s], rzs.at[s], rzr.at[s], dev(x, y, z + zoff(s, c), c))
-
-    def rx_copy(d):
-        return rcopy(dqs.at[d], qin.at[d], rxs.at[d], rxr.at[d], dev(x + d, y, z, c))
+        return rcopy(zb.at[s], zin.at[s], ss.at[23], cr.at[3], dev(x, y, z + zoff(s, c), c))
+
+    def rx_copy(d, half):
+        rows = pl.ds(64 * half, 64)
+        return rcopy(dqs.at[d, rows], qin.at[d, rows], ss.at[24], cr.at[4], dev(x + d, y, z, c))
+
+    def query_half(half):
+        for i in (2, 1, 3, 0):
+            tile = dqt[half, :, pl.ds(i * HD, HD)].T.astype(BF)
+            for h in range(2):
+                dqs[i, pl.ds(64 * half, 64), pl.ds(HD * h, HD)] = tile[64 * h : 64 * h + 64]
+            if i:
+                rx_copy(i, half).start()
 
     def presum(s):
         rs_copy(s).wait_recv()
@@ -248,6 +256,12 @@
         presum(s)
         ra_top(s).start()
         ra_bot(s).start()
+
+    def stage_direct(s):
+        presum(s)
+        ro_copy(s).start()
+        rb_up(s).start()
+        rb_down(s).start()
 
     def stage_b(s):
         ra_top(s).wait_recv()
@@ -262,75 +276,98 @@
         rb_down(s).wait_recv()
         return dkv[s, c, 0] + sib[s, 0].astype(F32) + ra[s].astype(F32) + rb[s].astype(F32)
 
+    def to_owner(s, direct=False):
+        t = own_sum(s)
+        if direct:
+            ro_copy(s).wait_recv()
+            t = t + rc[s - DIRECT].astype(F32)
+        zb[s] = t.astype(BF)
+        rz_copy(s).start()
+
     full_up(0).start()
     full_down(0).start()
     opp0.start()
     for s in range(1, 8):
+        pz_copy(s).start()
+    for n in (0, 2, 1, 3):
+        x_copy(n).start()
+    for s in range(1, 8):
         z_copy(s).start()
-    for n in range(4):
-        x_copy(n).start()
     for d in (1, 2, 3):
         m_copy(d).start()
-        ky_copy(0, d).start()
-    for s in range(1, 8):
-        pz_copy(s).start()
     dqt[...] = jnp.zeros_like(dqt)
     stage_full(1)
     full_up(0).wait_recv()
     full_down(0).wait_recv()
     opp0.wait_recv()
-    sib_rest(0, c).start()
+    sib_rest(0).start()
     x_copy(0).wait_recv()
     x_copy(4).start()
     x_copy(2).wait_recv()
     x_copy(5).start()
     stage_full(2)
+    all_of(kp.at[0, pl.ds(1, 7)], cr.at[0]).wait()
+    for d in (1, 2, 3):
+        ky_copy(d).start()
+    stage_full(3)
     stage_half(1)
-    stage_full(3)
-    for d in (1, 2, 3):
-        m_copy(d).wait_recv()
+    stage_full(4)
+    stage_half(2)
+    stage_full(5)
+    all_of(sm.at[rest], cr.at[2]).wait()
     prepare_rows(sm, rw)
     for n in (1, 3, 4, 5):
         x_copy(n).wait_recv()
+    stage_half(3)
+    stage_sib(1)
+    all_of(kp.at[rest], cr.at[1]).wait()
 
     def slot(s, carry):
+        @pl.when(s < 2)
+        def _():
+            stage_full(s + 6)
+
         @pl.when(s < 4)
         def _():
-            stage_full(s + 4)
+            stage_half(s + 4)
+
+        @pl.when((s >= 2) & (s < DIRECT + 2))
+        def _():
+            stage_a(s - 2)
+
+        @pl.when(s >= DIRECT + 2)
+        def _():
+            stage_direct(s - 2)
+
+        @pl.when(s >= 4)
+        def _():
+            stage_b(s - 4)
+
+        @pl.when(s == 6)
+        def _():
+            tot0[...] = own_sum(0)
+
+        @pl.when(s == 7)
+        def _():
+            to_owner(1)
+
+        @pl.when(s > 0)
+        def _():
+            all_of(kv.at[1 - c, s], br.at[s]).wait()
+
+        @pl.when(s == 0)
+        def _():
+            all_of(kv.at[1 - c, 0, rest], br.at[0]).wait()
+
+        key_half(s, 0, qx, rw, kv, kp, dkv, dqt)
 
         @pl.when(s < 6)
         def _():
-            stage_half(s + 2)
-
-        @pl.when(s < 7)
-        def _():
-            stage_sib(s + 1)
-
-        @pl.when(s > 0)
-        def _():
-            sib_own(s, 1 - c).wait_recv()
-
-        sib_rest(s, 1 - c).wait_recv()
-        for d in (1, 2, 3):
-            ky_copy(s, d).wait_recv()
-        key_half(s, 0, qx, rw, kv, kp, dkv, dqt)
-
-        @pl.when(s > 0)
-        def _():
-            stage_a(s - 1)
-
-        @pl.when(s > 1)
-        def _():
-            stage_b(s - 2)
-
-        @pl.when(s == 3)
-        def _():
-            tot0[...] = own_sum(0)
-
-        @pl.when(s > 3)
-        def _():
-            zb[s - 3] = own_sum(s - 3).astype(BF)
-            rz_copy(s - 3).start()
+            stage_sib(s + 2)
+
+        @pl.when(s == 7)
+        def _():
+            query_half(0)
 
         key_half(s, 1, qx, rw, kv, kp, dkv, dqt)
         so[s] = dkv[s, 1 - c].astype(BF)
@@ -338,88 +375,55 @@
         return carry
 
     lax.fori_loop(0, 8, slot, 0)
-    for i in (2, 1, 3, 0):
-        for half in range(2):
-            tile = dqt[half, :, pl.ds(i * HD, HD)].T.astype(BF)
-            for h in range(2):
-                dqs[i, pl.ds(64 * half, 64), pl.ds(HD * h, HD)] = tile[64 * h : 64 * h + 64]
-        if i:
-            rx_copy(i).start()
-    presum(7)
-    opp7.start()
-    rb_up(7).start()
-    rb_down(7).start()
-    stage_b(6)
-
-    def to_owner(s):
-        zb[s] = own_sum(s).astype(BF)
-        rz_copy(s).start()
-
-    to_owner(5)
-    opp7.wait_recv()
-    zb[7] = (own_sum(7) + rc[...].astype(F32)).astype(BF)
-    rz_copy(7).start()
-    to_owner(6)
+    query_half(1)
+    stage_direct(6)
+    stage_b(4)
+    to_owner(2)
+    to_owner(3)
+    stage_direct(7)
+    to_owner(5, True)
+    to_owner(4)
+    to_owner(6, True)
+    all_of(kv.at[c, pl.ds(1, 7), 0], ss.at[0]).wait()
+    all_of(kp.at[0, pl.ds(1, 7)], ss.at[1]).wait()
+    all_of(kp.at[rest], ss.at[2]).wait()
+    all_of(kv.at[c, :, 0], ss.at[3]).wait()
+    all_of(kv.at[c, :, 0], ss.at[4]).wait()
+    all_of(kv.at[c, pl.ds(1, 7), 2, top], ss.at[5]).wait()
+    all_of(kv.at[c, pl.ds(1, 7), 2, bot], ss.at[6]).wait()
+    opp0.wait_send()
+    all_of(kv.at[c, pl.ds(1, 7), 0], ss.at[8]).wait()
+    all_of(kv.at[c, :, rest], ss.at[9]).wait()
+    for n in range(6):
+        x_copy(n).wait_send()
+    all_of(sm.at[rest], ss.at[16]).wait()
+    to_owner(7, True)
+    all_of(qin.at[rest], cr.at[4]).wait()
     qsum = dqs[0].astype(F32)
-    for d in (1, 3, 2):
-        rx_copy(d).wait_recv()
+    for d in (1, 2, 3):
         qsum = qsum + qin[d].astype(F32)
     qfin[0] = qsum.astype(BF)
-    sq = rcopy(qfin.at[0], qfin.at[1], fs.at[0], fr.at[0], other)
+    sq = rcopy(qfin.at[0], qfin.at[1], ss.at[25], cr.at[5], other)
     sq.start()
+    all_of(zin.at[pl.ds(1, 7)], cr.at[3]).wait()
     tot = tot0[...]
     for s in range(1, 8):
-        rz_copy(s).wait_recv()
         tot = tot + zin[s].astype(F32)
     fin[0] = tot.astype(BF)
-    sk = rcopy(fin.at[0], fin.at[1], fs.at[1], fr.at[1], other)
+    sk = rcopy(fin.at[0], fin.at[1], ss.at[26], cr.at[6], other)
     sk.start()
     low = c == 0
     sq.wait_recv()
     gq_ref[:, 0:256] = jnp.where(low, qfin[0], qfin[1])
     gq_ref[:, 256:512] = jnp.where(low, qfin[1], qfin[0])
-    for n in range(6):
-        x_copy(n).wait_send()
-    for d in (1, 2, 3):
-        m_copy(d).wait_send()
-        rx_copy(d).wait_send()
-    full_up(0).wait_send()
-    full_down(0).wait_send()
-    opp0.wait_send()
-    sib_rest(0, c).wait_send()
-    rs_copy(0).wait_send()
-    for d in (1, 2, 3):
-        ky_copy(0, d).wait_send()
-    opp7.wait_send()
-    ra_top(0).wait_send()
-    ra_bot(0).wait_send()
-    rb_up(0).wait_send()
-    rb_down(0).wait_send()
-
-    def drain(s, carry):
-        z_copy(s).wait_send()
-        pz_copy(s).wait_send()
-        full_up(s).wait_send()
-        full_down(s).wait_send()
-        half_up(s).wait_send()
-        half_down(s).wait_send()
-        sib_own(s, c).wait_send()
-        sib_rest(s, c).wait_send()
-        for d in (1, 2, 3):
-            ky_copy(s, d).wait_send()
-        rs_copy(s).wait_send()
-        rb_up(s).wait_send()
-        rb_down(s).wait_send()
-        rz_copy(s).wait_send()
-
-        @pl.when(s < 7)
-        def _():
-            ra_top(s).wait_send()
-            ra_bot(s).wait_send()
-
-        return carry
-
-    lax.fori_loop(1, 8, drain, 0)
+    all_of(sib, ss.at[17]).wait()
+    all_of(fa.at[pl.ds(0, DIRECT)], ss.at[18]).wait()
+    all_of(fb.at[pl.ds(0, DIRECT)], ss.at[19]).wait()
+    all_of(ra, ss.at[20]).wait()
+    all_of(rb, ss.at[21]).wait()
+    all_of(rc, ss.at[22]).wait()
+    all_of(zin.at[pl.ds(1, 7)], ss.at[23]).wait()
+    all_of(qin.at[rest], ss.at[24]).wait()
     sq.wait_send()
     sk.wait()
     gk_ref[...] = jnp.where(low, fin[0], fin[1])
@@ -455,7 +459,7 @@
             pltpu.VMEM((8, 64, 128), BF),
             pltpu.VMEM((8, 128, 128), BF),
             pltpu.VMEM((8, 128, 128), BF),
-            pltpu.VMEM((128, 128), BF),
+            pltpu.VMEM((8 - DIRECT, 128, 128), BF),
             pltpu.VMEM((8, 128, 128), BF),
             pltpu.VMEM((8, 128, 128), BF),
             pltpu.VMEM((128, 128), F32),
@@ -463,10 +467,7 @@
             pltpu.VMEM((4, 128, 256), BF),
             pltpu.VMEM((2, 128, 128), BF),
             pltpu.VMEM((2, 128, 256), BF),
-            DMA((8,)), DMA((8,)), DMA((8,)), DMA((8,)), DMA((8, 4)), DMA((8, 4)), DMA((8, 4)), DMA((8, 4)),
-            DMA((8, 2)), DMA((8, 2)), DMA((6,)), DMA((6,)), DMA((4,)), DMA((4,)),
-            DMA((8,)), DMA((8,)), DMA((8, 4)), DMA((8, 4)), DMA((8,)), DMA((8,)), DMA((4,)), DMA((4,)),
-            DMA((2,)), DMA((2,)),
+            DMA((27,)), DMA((8,)), DMA((8, 4)), DMA((8,)), DMA((6,)), DMA((7,)), DMA((8,)), DMA((8, 4)),
         ],
         compiler_params=pltpu.CompilerParams(collective_id=0, has_side_effects=True),
         name="attention_grad",

time: 67.3 us -> 59.2 us (0.88)
  Pallas kernels: 63 us -> 55.4 us
    pallas_call x1, Pallas kernels: 63 us -> 55.4 us  [per_device(): pl.pallas_call(fused_kernel, out_shape=(jax.ShapeDtypeStruct((128, 512),...]
where the time goes in v3:
time: 59.2 us; the launch traced here: 59 us
  Pallas kernels  55.4 us (94%)
  local copies, waits for them, and re-layouts  2.96 us (5%)
  between operations  0.65 us (1%)
    pallas_call x1, Pallas kernels, per_device(): pl.pallas_call(fused_kernel, out_shape=(jax.ShapeDtypeStruct((128, 512),...  55.4 us
    unnamed x7, local copies, waits for them, and re-layouts  2.96 us

profile of v3, /device:TPU:1, one launch (start us, length us, event | category | flops | bytes accessed | tf_op | source)
XLA Modules:
  0.0 59.0 jit_solution(5320708134040144864)
XLA Ops:
  0.6 55.4 %attention_grad.1 = (bf16[128,512]{1,0:T(8,128)(2,1)}, bf16[128,128]{1,0:T(8,128)(2,1)}, bf16[128,128]{1,0:T(8,128)(2,1)}) custom-call(bf16[128,512]{1,0:T(8,128)(2,1)} %q_ref.1, bf16[128,128]{1,0:T(8,128)(2,1)} %k_ref.1, bf16[128,128]{1,0:T(8,128)(2,1)} %v_ref.1, bf16[128,512]{1,0:T(8,128)(2,1)} %o_ref.1, bf16[128,512]{1,0:T(8,128)(2,1)} %do_ref.1, ...), custom_call_target="tpu_custom_call" | custom-call | tf_op jit(solution)/shard_map/attention_grad/pallas_call | solution.py:438
  56.0 0.0 copy-start.1
  56.0 1.6 %copy.13 = bf16[128,512]{1,0:T(8,128)(2,1)} copy(bf16[128,512]{1,0:T(8,128)(2,1)} %get-tuple-element.6) | data formatting | bytes 262144
  57.6 0.0 copy-done.1
  57.6 0.0 copy-start
  57.6 0.6 %copy.14 = bf16[128,128]{1,0:T(8,128)(2,1)} copy(bf16[128,128]{1,0:T(8,128)(2,1)S(1)} %copy-done.1) | data formatting | bytes 65536
  58.2 0.2 copy-done
  58.4 0.6 %copy.15 = bf16[128,128]{1,0:T(8,128)(2,1)} copy(bf16[128,128]{1,0:T(8,128)(2,1)S(1)} %copy-done) | data formatting | bytes 65536
Async XLA Ops:
  56.0 1.6 %copy-start.1 = (bf16[128,128]{1,0:T(8,128)(2,1)S(1)}, bf16[128,128]{1,0:T(8,128)(2,1)}, u32[]{:S(2)}) copy-start(bf16[128,128]{1,0:T(8,128)(2,1)} %get-tuple-element.7) | copy-start | bytes 98308
  57.6 0.8 %copy-start = (bf16[128,128]{1,0:T(8,128)(2,1)S(1)}, bf16[128,128]{1,0:T(8,128)(2,1)}, u32[]{:S(2)}) copy-start(bf16[128,128]{1,0:T(8,128)(2,1)} %get-tuple-element.8) | copy-start | bytes 98308

commit v4 on v3

v4 whole, which is shorter than its diff:
```python
import math

import jax
import jax.numpy as jnp
from jax import lax
from jax.experimental import pallas as pl
from jax.experimental.pallas import tpu as pltpu
from jax.sharding import PartitionSpec as P

MESH = pl.DeviceIdType.MESH
BF = jnp.bfloat16
F32 = jnp.float32
HD = 128
SCALE = HD ** (-0.5)
LOG2E = math.log2(math.e)
BIG = 1e30


def coords():
    b = lax.axis_index("blk")
    r = lax.axis_index("rep")
    x = b // 32
    y = b % 4
    z = (r // 2) * 8 + (b // 4) % 8
    return x, y, z, r % 2


def dev(x, y, z, c):
    xx = (x + 4) % 4
    yy = (y + 4) % 4
    zz = (z + 16) % 16
    return ((xx * 8 + zz % 8) * 4 + yy, (zz // 8) * 2 + c)


def entry_barrier(x, y, z, c):
    group = [dev(x, y, z, 1 - c)]
    for d in (1, 2, 3):
        group.append(dev(x + d, y, z, c))
        group.append(dev(x, y + d, z, c))
    for o in (1, 2, 3, -1, -2, -3):
        group.append(dev(x, y, z + o, c))
    barrier = pltpu.get_barrier_semaphore()
    for d in group:
        pl.semaphore_signal(barrier, inc=1, device_id=d, device_id_type=MESH)
    return barrier, len(group)


def rcopy(src, dst, ssem, rsem, device):
    return pltpu.make_async_remote_copy(
        src_ref=src, dst_ref=dst, send_sem=ssem, recv_sem=rsem, device_id=device, device_id_type=MESH
    )


def nt(a, b):
    return lax.dot_general(a, b, (((1,), (1,)), ((), ())), preferred_element_type=F32)


def nn(a, b):
    return lax.dot_general(a, b, (((1,), (0,)), ((), ())), preferred_element_type=F32)


def prepare_rows(sm_ref, rw, blocks):
    for i in blocks:
        rw[:, pl.ds(i * HD, HD)] = sm_ref[i]


def key_half(s, kh, u, qx, rw, kv_ref, kp_ref, dkv, dqt):
    rows = pl.ds(64 * kh, 64)
    kc = kv_ref[0, s, :, rows, :].reshape(256, HD)
    vc = kv_ref[1, s, :, rows, :].reshape(256, HD)
    kt = kc.T
    dk = jnp.zeros((256, HD), F32)
    dv = jnp.zeros((256, HD), F32)
    for half in ((0, 1) if kh == 0 else (1,)):
        for g in (2 * u, 2 * u + 1):
            ls = pl.ds(256 * g, 256)
            lse = rw[half : half + 1, ls]
            dlt = rw[2 + half : 3 + half, ls]
            if kh != half:
                le = jnp.broadcast_to(lse, (4, 256))
            else:
                qp = rw[4:5, ls].astype(jnp.int32) * 32768 + rw[5:6, ls].astype(jnp.int32)
                parts = []
                for yb in range(4):
                    kp = jnp.broadcast_to(kp_ref[yb, s][:, 0:1], (1, 256))
                    seen = kp <= qp if kh == 0 else kp >= qp
                    parts.append(jnp.where(seen, lse, BIG))
                le = jnp.concatenate(parts, axis=0)
            qg = qx[0, half, 2 * g : 2 * g + 2].reshape(256, HD)
            dg = qx[1, half, 2 * g : 2 * g + 2].reshape(256, HD)
            sc = nt(kc, qg).reshape(4, 64, 256)
            dp = nt(vc, dg)
            t = (sc * (SCALE * LOG2E) - le[:, None, :]).reshape(256, 256)
            if kh == half and g == 0:
                ri = lax.broadcasted_iota(jnp.int32, (64, HD), 0)
                li = lax.broadcasted_iota(jnp.int32, (64, HD), 1)
                own = jnp.where(ri <= li % 64 + 64 * s, t[:64, :HD], -BIG)
                t = jnp.concatenate([jnp.concatenate([own, t[:64, HD:]], axis=1), t[64:]], axis=0)
            p = jnp.exp2(t)
            ds = (p * (dp * SCALE - dlt)).astype(BF)
            dv = dv + nn(p.astype(BF), dg)
            dk = dk + nn(ds, qg)
            dqt[half, :, ls] += nn(kt, ds)
    if u:
        dk = dk + dkv[s, 0, :, rows, :].reshape(256, HD)
        dv = dv + dkv[s, 1, :, rows, :].reshape(256, HD)
    dkv[s, 0, :, rows, :] = dk.reshape(4, 64, HD)
    dkv[s, 1, :, rows, :] = dv.reshape(4, 64, HD)


def fused_kernel(
    q_ref, k_ref, v_ref, o_ref, do_ref, lse_ref, pos_ref,
    gq_ref, gk_ref, gv_ref,
    qx, sm, kv, kp, rw, dqt, dkv, so, sib, acc, fa, fb, ra, rb, rc, zb, zin, tot0, dqs, qin, qb, qp, fin, qfin,
    ov, lv, pv, ss, zr, yr, br, xr, cr, rbr, ryr, ir,
):
    x, y, z, c = coords()
    barrier, count = entry_barrier(x, y, z, c)
    other = dev(x, y, z, 1 - c)
    up, down = dev(x, y + 1, z, c), dev(x, y - 1, z, c)
    right, left = dev(x + 1, y, z, c), dev(x - 1, y, z, c)
    away = 2 * (z % 2) - 1
    partner = dev(x, y, z - away, c)
    top, bot = pl.ds(0, 64), pl.ds(64, 64)
    rest = pl.ds(1, 3)
    col = pl.multiple_of(c * 256, 256)

    def all_of(ref, sem):
        return pltpu.make_async_copy(ref, ref, sem)

    pltpu.make_async_copy(k_ref, kv.at[0, 0, 0], ir.at[0]).start()
    pltpu.make_async_copy(v_ref, kv.at[1, 0, 0], ir.at[1]).start()
    for n, ref, dst in ((2, do_ref, qx.at[1, :, 0]), (3, o_ref, ov), (4, q_ref, qx.at[0, :, 0])):
        for half in range(2):
            for h in range(2):
                pltpu.make_async_copy(
                    ref.at[pl.ds(64 * half, 64), pl.ds(col + HD * h, HD)], dst.at[half, pl.ds(64 * h, 64)], ir.at[n]
                ).start()
    pltpu.make_async_copy(lse_ref, lv, ir.at[5]).start()
    pltpu.make_async_copy(pos_ref, pv, ir.at[6]).start()
    all_of(qx.at[1, :, 0], ir.at[2]).wait()
    all_of(ov, ir.at[3]).wait()
    all_of(lv, ir.at[5]).wait()
    all_of(pv, ir.at[6]).wait()
    sel = lax.broadcasted_iota(jnp.int32, (1, HD), 1) < 64
    l0 = lv[pl.ds(2 * c, 1), :] * LOG2E
    l1 = lv[pl.ds(2 * c + 1, 1), :] * LOG2E
    rows = [jnp.where(sel, l0, pltpu.roll(l1, 64, 1)), jnp.where(sel, pltpu.roll(l0, 64, 1), l1)]
    for half in range(2):
        prod = qx[1, half, 0].astype(F32) * ov[half].astype(F32)
        total = jnp.sum(prod, axis=1, keepdims=True) * SCALE
        rows.append(jnp.broadcast_to(total, (HD, HD)).T[0:1, :])
    p = jnp.broadcast_to(pv[0:1, 0:1], (1, HD))
    rows.append((p // 32768).astype(F32))
    rows.append((p % 32768).astype(F32))
    rows.append(jnp.zeros((2, HD), F32))
    sm[0] = jnp.concatenate(rows, axis=0)
    kp[0, 0] = pv[...]
    dqt[...] = jnp.zeros_like(dqt)
    all_of(kv.at[0, 0, 0], ir.at[0]).wait()
    all_of(kv.at[1, 0, 0], ir.at[1]).wait()
    all_of(qx.at[0, :, 0], ir.at[4]).wait()
    pl.semaphore_wait(barrier, count)

    def z_copy(s):
        to = z + s * away if s % 2 else z - s * away
        return rcopy(kv.at[c, 0, 0], kv.at[c, s, 0], ss.at[0], zr.at[s], dev(x, y, to, c))

    def pz_copy(s):
        to = z + s * away if s % 2 else z - s * away
        return rcopy(kp.at[0, 0], kp.at[0, s], ss.at[1], cr.at[0], dev(x, y, to, c))

    def ky_copy(d):
        return rcopy(kp.at[0], kp.at[d], ss.at[2], cr.at[1], dev(x, y - d, z, c))

    def full_up(s):
        return rcopy(kv.at[c, s, 0], kv.at[c, s, 3], ss.at[3], yr.at[s, 0], up)

    def full_down(s):
        return rcopy(kv.at[c, s, 0], kv.at[c, s, 1], ss.at[4], yr.at[s, 1], down)

    def half_up(s):
        return rcopy(kv.at[c, s, 3, top], kv.at[c, s, 2, top], ss.at[5], yr.at[s, 2], up)

    def half_down(s):
        return rcopy(kv.at[c, s, 1, bot], kv.at[c, s, 2, bot], ss.at[6], yr.at[s, 3], down)

    opp0 = rcopy(kv.at[c, 0, 0], kv.at[c, 0, 2], ss.at[7], yr.at[0, 2], dev(x, y + 2, z, c))

    def sib_own(s):
        return rcopy(kv.at[c, s, 0], kv.at[c, s, 0], ss.at[8], br.at[s], other)

    def sib_rest(s):
        return rcopy(kv.at[c, s, rest], kv.at[c, s, rest], ss.at[9], br.at[s], other)

    def x_copy(n, u):
        src, dst, half, to = (
            (0, 3, 0, right), (0, 3, 1, right), (0, 1, 1, left), (0, 1, 0, left), (3, 2, 0, right), (1, 2, 1, left)
        )[n]
        return rcopy(
            qx.at[:, half, src + 4 * u], qx.at[:, half, dst + 4 * u], ss.at[10 + n + 18 * u], xr.at[u, n], to
        )

    def zq_copy(half):
        return rcopy(qx.at[:, half, 0], qx.at[:, half, 4], ss.at[34], cr.at[8 + half], partner)

    def m_copy(d):
        return rcopy(sm.at[0], sm.at[d], ss.at[16], cr.at[2], dev(x - d, y, z, c))

    mz_copy = rcopy(sm.at[0], sm.at[4], ss.at[35], cr.at[10], partner)

    def m2_copy(d):
        return rcopy(sm.at[4], sm.at[4 + d], ss.at[36], cr.at[11], dev(x - d, y, z, c))

    def stage_full(s):
        z_copy(s).wait_recv()
        full_up(s).start()
        full_down(s).start()
        sib_own(s).start()

    def stage_half(s):
        full_up(s).wait_recv()
        half_up(s).start()
        full_down(s).wait_recv()
        half_down(s).start()

    def stage_sib(s):
        half_up(s).wait_recv()
        half_down(s).wait_recv()
        sib_rest(s).start()

    def rs_copy(s):
        return rcopy(so.at[s], sib.at[s], ss.at[17], rbr.at[s], other)

    def ra_top(s):
        return rcopy(acc.at[s, 2, top], fa.at[s - 2], ss.at[18], ryr.at[s, 0], up)

    def ra_bot(s):
        return rcopy(acc.at[s, 2, bot], fb.at[s - 2], ss.at[19], ryr.at[s, 1], down)

    def rb_up(s):
        return rcopy(acc.at[s, 1], ra.at[s], ss.at[20], ryr.at[s, 2], up)

    def rb_down(s):
        return rcopy(acc.at[s, 3], rb.at[s], ss.at[21], ryr.at[s, 3], down)

    def ro_copy(s):
        return rcopy(acc.at[s, 2], rc.at[s], ss.at[22], ryr.at[s, 0], dev(x, y + 2, z, c))

    def rz_copy(s):
        return rcopy(zb.at[s], zin.at[s], ss.at[23], cr.at[3], dev(x, y, z + s * away, c))

    def rx_copy(d, half, u):
        rows = pl.ds(64 * half, 64)
        got = cr.at[12 + half] if u else cr.at[4]
        return rcopy(
            dqs.at[d + 4 * u, rows], qin.at[d + 4 * u, rows], ss.at[37 if u else 24], got, dev(x + d, y, z, c)
        )

    def rp_copy(half):
        rows = pl.ds(64 * half, 64)
        return rcopy(qb.at[rows], qp.at[rows], ss.at[38], cr.at[14 + half], partner)

    def share(half):
        rows = pl.ds(64 * half, 64)
        return rcopy(qfin.at[0, rows], qfin.at[1, rows], ss.at[25 + half], cr.at[5 + half], other)

    def query_half(half, u):
        for i in (2, 1, 3, 0):
            tile = dqt[half, :, pl.ds((i + 4 * u) * HD, HD)].T.astype(BF)
            for h in range(2):
                dqs[i + 4 * u, pl.ds(64 * half, 64), pl.ds(HD * h, HD)] = tile[64 * h : 64 * h + 64]
            if i:
                rx_copy(i, half, u).start()

    def presum(s):
        rs_copy(s).wait_recv()
        for d in (2, 1, 3):
            acc[s, d] = (dkv[s, c, d] + sib[s, d].astype(F32)).astype(BF)

    def stage_a(s):
        presum(s)
        ra_top(s).start()
        ra_bot(s).start()

    def stage_direct(s):
        presum(s)
        ro_copy(s).start()
        rb_up(s).start()
        rb_down(s).start()

    def stage_b(s):
        ra_top(s).wait_recv()
        acc[s, 1, top] = (acc[s, 1, top].astype(F32) + fa[s - 2].astype(F32)).astype(BF)
        rb_up(s).start()
        ra_bot(s).wait_recv()
        acc[s, 3, bot] = (acc[s, 3, bot].astype(F32) + fb[s - 2].astype(F32)).astype(BF)
        rb_down(s).start()

    def own_sum(s):
        rb_up(s).wait_recv()
        rb_down(s).wait_recv()
        return dkv[s, c, 0] + sib[s, 0].astype(F32) + ra[s].astype(F32) + rb[s].astype(F32)

    def direct_sum(s):
        t = own_sum(s)
        ro_copy(s).wait_recv()
        return t + rc[s].astype(F32)

    def to_owner(s, total):
        zb[s] = total.astype(BF)
        rz_copy(s).start()

    full_up(0).start()
    full_down(0).start()
    opp0.start()
    for s in (1, 2, 3):
        pz_copy(s).start()
    for n in (0, 2, 1, 3):
        x_copy(n, 0).start()
    for s in (1, 2, 3):
        z_copy(s).start()
    for half in range(2):
        zq_copy(half).start()
    for d in (1, 2, 3):
        m_copy(d).start()
    mz_copy.start()
    stage_full(1)
    full_up(0).wait_recv()
    full_down(0).wait_recv()
    opp0.wait_recv()
    sib_rest(0).start()
    x_copy(0, 0).wait_recv()
    x_copy(4, 0).start()
    x_copy(2, 0).wait_recv()
    x_copy(5, 0).start()
    stage_full(2)
    all_of(kp.at[0, rest], cr.at[0]).wait()
    for d in (1, 2, 3):
        ky_copy(d).start()
    zq_copy(0).wait_recv()
    x_copy(0, 1).start()
    stage_full(3)
    stage_half(1)
    zq_copy(1).wait_recv()
    for n in (2, 1, 3):
        x_copy(n, 1).start()
    all_of(sm.at[4], cr.at[10]).wait()
    for d in (1, 2, 3):
        m2_copy(d).start()
    stage_half(2)
    all_of(sm.at[rest], cr.at[2]).wait()
    prepare_rows(sm, rw, range(4))
    for n in (1, 3, 4, 5):
        x_copy(n, 0).wait_recv()
    stage_half(3)
    stage_sib(1)
    all_of(kp.at[rest], cr.at[1]).wait()

    def own_queries(s, carry):
        @pl.when(s == 1)
        def _():
            x_copy(0, 1).wait_recv()
            x_copy(4, 1).start()
            x_copy(2, 1).wait_recv()
            x_copy(5, 1).start()

        @pl.when(s > 0)
        def _():
            all_of(kv.at[1 - c, s], br.at[s]).wait()

        @pl.when(s == 0)
        def _():
            all_of(kv.at[1 - c, 0, rest], br.at[0]).wait()

        key_half(s, 0, 0, qx, rw, kv, kp, dkv, dqt)

        @pl.when(s < 2)
        def _():
            stage_sib(s + 2)

        key_half(s, 1, 0, qx, rw, kv, kp, dkv, dqt)
        return carry

    lax.fori_loop(0, 4, own_queries, 0)
    for half in range(2):
        query_half(half, 0)
    all_of(sm.at[pl.ds(5, 3)], cr.at[11]).wait()
    prepare_rows(sm, rw, range(4, 8))
    for n in (1, 3, 4, 5):
        x_copy(n, 1).wait_recv()

    def partner_queries(t, carry):
        s = 3 - t

        @pl.when(t >= 2)
        def _():
            stage_a(s + 2)

        key_half(s, 0, 1, qx, rw, kv, kp, dkv, dqt)

        @pl.when(t == 3)
        def _():
            query_half(0, 1)

        key_half(s, 1, 1, qx, rw, kv, kp, dkv, dqt)
        so[s] = dkv[s, 1 - c].astype(BF)
        rs_copy(s).start()
        return carry

    lax.fori_loop(0, 4, partner_queries, 0)
    query_half(1, 1)
    stage_direct(1)
    stage_b(3)
    stage_b(2)
    stage_direct(0)
    all_of(kv.at[c, rest, 0], ss.at[0]).wait()
    all_of(kp.at[0, rest], ss.at[1]).wait()
    all_of(kp.at[rest], ss.at[2]).wait()
    all_of(kv.at[c, :, 0], ss.at[3]).wait()
    all_of(kv.at[c, :, 0], ss.at[4]).wait()
    all_of(kv.at[c, rest, 2, top], ss.at[5]).wait()
    all_of(kv.at[c, rest, 2, bot], ss.at[6]).wait()
    opp0.wait_send()
    all_of(kv.at[c, rest, 0], ss.at[8]).wait()
    all_of(kv.at[c, :, rest], ss.at[9]).wait()
    for u in range(2):
        for n in range(6):
            x_copy(n, u).wait_send()
    all_of(qx.at[:, :, 4], ss.at[34]).wait()
    all_of(sm.at[rest], ss.at[16]).wait()
    all_of(sm.at[4], ss.at[35]).wait()
    all_of(sm.at[pl.ds(5, 3)], ss.at[36]).wait()
    all_of(qin.at[rest], cr.at[4]).wait()
    qsum = dqs[0].astype(F32)
    for d in (1, 2, 3):
        qsum = qsum + qin[d].astype(F32)
    to_owner(3, own_sum(3))
    to_owner(1, direct_sum(1))
    to_owner(2, own_sum(2))
    tot0[...] = direct_sum(0)
    for half in range(2):
        rows = pl.ds(64 * half, 64)
        all_of(qin.at[pl.ds(5, 3), rows], cr.at[12 + half]).wait()
        psum = dqs[4, rows].astype(F32)
        for d in (1, 2, 3):
            psum = psum + qin[4 + d, rows].astype(F32)
        qb[rows] = psum.astype(BF)
        rp_copy(half).start()
    all_of(zin.at[rest], cr.at[3]).wait()
    tot = tot0[...]
    for s in (1, 2, 3):
        tot = tot + zin[s].astype(F32)
    fin[0] = tot.astype(BF)
    sk = rcopy(fin.at[0], fin.at[1], ss.at[27], cr.at[7], other)
    sk.start()
    for half in range(2):
        rows = pl.ds(64 * half, 64)
        rp_copy(half).wait_recv()
        qfin[0, rows] = (qsum[64 * half : 64 * half + 64] + qp[rows].astype(F32)).astype(BF)
        share(half).start()
    all_of(sib, ss.at[17]).wait()
    all_of(fa, ss.at[18]).wait()
    all_of(fb, ss.at[19]).wait()
    all_of(ra, ss.at[20]).wait()
    all_of(rb, ss.at[21]).wait()
    all_of(rc, ss.at[22]).wait()
    all_of(zin.at[rest], ss.at[23]).wait()
    all_of(qin.at[rest], ss.at[24]).wait()
    all_of(qin.at[pl.ds(5, 3)], ss.at[37]).wait()
    all_of(qp, ss.at[38]).wait()
    low = c == 0
    sk.wait()
    gk_ref[...] = jnp.where(low, fin[0], fin[1])
    gv_ref[...] = jnp.where(low, fin[1], fin[0])
    for half in range(2):
        share(half).wait()
    gq_ref[:, 0:256] = jnp.where(low, qfin[0], qfin[1])
    gq_ref[:, 256:512] = jnp.where(low, qfin[1], qfin[0])


def hand_on(a_ref, b_ref, c_ref, ao_ref, bo_ref, co_ref):
    ao_ref[...] = a_ref[...]
    bo_ref[...] = b_ref[...]
    co_ref[...] = c_ref[...]


VM = pl.BlockSpec(memory_space=pltpu.VMEM)
DMA = pltpu.SemaphoreType.DMA


def per_device(queries, keys, values, output, grad_out, lse, positions):
    partial = pl.pallas_call(
        fused_kernel,
        out_shape=(
            jax.ShapeDtypeStruct((128, 512), BF),
            jax.ShapeDtypeStruct((128, 128), BF),
            jax.ShapeDtypeStruct((128, 128), BF),
        ),
        in_specs=[pl.BlockSpec(memory_space=pltpu.HBM)] * 7,
        out_specs=(VM,) * 3,
        scratch_shapes=[
            pltpu.VMEM((2, 2, 8, 128, 128), BF),
            pltpu.VMEM((8, 8, 128), F32),
            pltpu.VMEM((2, 4, 4, 128, 128), BF),
            pltpu.VMEM((4, 4, 1, 128), jnp.int32),
            pltpu.VMEM((8, 1024), F32),
            pltpu.VMEM((2, 128, 1024), F32),
            pltpu.VMEM((4, 2, 4, 128, 128), F32),
            pltpu.VMEM((4, 4, 128, 128), BF),
            pltpu.VMEM((4, 4, 128, 128), BF),
            pltpu.VMEM((4, 4, 128, 128), BF),
            pltpu.VMEM((2, 64, 128), BF),
            pltpu.VMEM((2, 64, 128), BF),
            pltpu.VMEM((4, 128, 128), BF),
            pltpu.VMEM((4, 128, 128), BF),
            pltpu.VMEM((2, 128, 128), BF),
            pltpu.VMEM((4, 128, 128), BF),
            pltpu.VMEM((4, 128, 128), BF),
            pltpu.VMEM((128, 128), F32),
            pltpu.VMEM((8, 128, 256), BF),
            pltpu.VMEM((8, 128, 256), BF),
            pltpu.VMEM((128, 256), BF),
            pltpu.VMEM((128, 256), BF),
            pltpu.VMEM((2, 128, 128), BF),
            pltpu.VMEM((2, 128, 256), BF),
            pltpu.VMEM((2, 128, 128), BF),
            pltpu.VMEM((4, 128), F32),
            pltpu.VMEM((1, 128), jnp.int32),
            DMA((39,)), DMA((4,)), DMA((4, 4)), DMA((4,)), DMA((2, 6)), DMA((16,)), DMA((4,)), DMA((4, 4)), DMA((7,)),
        ],
        compiler_params=pltpu.CompilerParams(
            collective_id=0, has_side_effects=True
        ),
        name="attention_grad",
    )(queries, keys, values, output, grad_out, lse, positions.reshape(1, 128))
    return pl.pallas_call(
        hand_on,
        out_shape=tuple(jax.ShapeDtypeStruct(a.shape, a.dtype) for a in partial),
        in_specs=[VM] * 3,
        out_specs=(VM,) * 3,
        name="hand_on",
    )(*partial)


def solution(mesh):
    placed = (
        P("blk", None),
        P("blk", None),
        P("blk", None),
        P("blk", None),
        P("blk", None),
        P(None, "blk"),
        P("blk"),
    )
    return jax.shard_map(
        per_device,
        mesh=mesh,
        in_specs=placed,
        out_specs=(P("blk", None), P("blk", None), P("blk", None)),
        check_vma=False,
    )
```

time: 59.2 us -> 56.1 us (0.948)
  local copies, waits for them, and re-layouts: 2.96 us -> 0 us
    unnamed x7 -> x0, local copies, waits for them, and re-layouts: 2.96 us -> none
    pallas_call x1, Pallas kernels: 55.4 us -> 53.7 us  [per_device(): pl.pallas_call(fused_kernel, out_shape=(jax.ShapeDtypeStruct((128, 512),...]
    pallas_call x0 -> x1, Pallas kernels: none -> 1.6 us  [per_device(): pl.pallas_call(hand_on, out_shape=tuple((jax.ShapeDtypeStruct(a.shape, a....]
where the time goes in v4:
time: 56.1 us; the launch traced here: 55.9 us
  Pallas kernels  55.3 us (99%)
  between operations  0.64 us (1%)
    pallas_call x1, Pallas kernels, per_device(): pl.pallas_call(fused_kernel, out_shape=(jax.ShapeDtypeStruct((128, 512),...  53.7 us
    pallas_call x1, Pallas kernels, per_device(): pl.pallas_call(hand_on, out_shape=tuple((jax.ShapeDtypeStruct(a.shape, a....  1.6 us

profile of v4, /device:TPU:1, one launch (start us, length us, event | category | flops | bytes accessed | tf_op | source)
XLA Modules:
  0.0 55.9 jit_solution(17524829450300436671)
XLA Ops:
  0.6 53.7 %attention_grad.1 = (bf16[128,512]{1,0:T(8,128)(2,1)}, bf16[128,128]{1,0:T(8,128)(2,1)}, bf16[128,128]{1,0:T(8,128)(2,1)}) custom-call(bf16[128,512]{1,0:T(8,128)(2,1)} %q_ref.1, bf16[128,128]{1,0:T(8,128)(2,1)} %k_ref.1, bf16[128,128]{1,0:T(8,128)(2,1)} %v_ref.1, bf16[128,512]{1,0:T(8,128)(2,1)} %o_ref.1, bf16[128,512]{1,0:T(8,128)(2,1)} %do_ref.1, ...), custom_call_target="tpu_custom_call" | custom-call | tf_op jit(solution)/shard_map/attention_grad/pallas_call | solution.py:493
  54.3 1.6 %hand_on.1 = (bf16[128,512]{1,0:T(8,128)(2,1)}, bf16[128,128]{1,0:T(8,128)(2,1)}, bf16[128,128]{1,0:T(8,128)(2,1)}) custom-call(bf16[128,512]{1,0:T(8,128)(2,1)} %get-tuple-element.6.a_ref, bf16[128,128]{1,0:T(8,128)(2,1)} %get-tuple-element.7.b_ref, bf16[128,128]{1,0:T(8,128)(2,1)} %get-tuple-element.8.c_ref), custom_call_target="tpu_custom_call" | custom-call | tf_op jit(solution)/shard_map/hand_on/pallas_call | solution.py:537

commit v5 on v4

--- a/solution.py
+++ b/solution.py
@@ -530,15 +530,21 @@
             DMA((39,)), DMA((4,)), DMA((4, 4)), DMA((4,)), DMA((2, 6)), DMA((16,)), DMA((4,)), DMA((4, 4)), DMA((7,)),
         ],
         compiler_params=pltpu.CompilerParams(
-            collective_id=0, has_side_effects=True
+            collective_id=0, has_side_effects=True, vmem_limit_bytes=24 * 2**20
         ),
         name="attention_grad",
-    )(queries, keys, values, output, grad_out, lse, positions.reshape(1, 128))
+    )(
+        *(
+            pltpu.with_memory_space_constraint(a, pltpu.HBM)
+            for a in (queries, keys, values, output, grad_out, lse, positions.reshape(1, 128))
+        )
+    )
     return pl.pallas_call(
         hand_on,
         out_shape=tuple(jax.ShapeDtypeStruct(a.shape, a.dtype) for a in partial),
         in_specs=[VM] * 3,
         out_specs=(VM,) * 3,
+        compiler_params=pltpu.CompilerParams(vmem_limit_bytes=4 * 2**20),
         name="hand_on",
     )(*partial)
 

time: 56.1 us -> 54.5 us (0.971)
  Pallas kernels: 55.3 us -> 53.7 us
    pallas_call x1, Pallas kernels: 1.6 us -> 0.68 us  [per_device(): pl.pallas_call(hand_on, out_shape=tuple((jax.ShapeDtypeStruct(a.shape, a....]
    pallas_call x1, Pallas kernels: 53.7 us -> 53 us  [per_device(): pl.pallas_call(fused_kernel, out_shape=(jax.ShapeDtypeStruct((128, 512),...]
where the time goes in v5:
time: 54.5 us; the launch traced here: 54.3 us
  Pallas kernels  53.7 us (99%)
  between operations  0.64 us (1%)
    pallas_call x1, Pallas kernels, per_device(): pl.pallas_call(fused_kernel, out_shape=(jax.ShapeDtypeStruct((128, 512),...  53 us

profile of v5, /device:TPU:1, one launch (start us, length us, event | category | flops | bytes accessed | tf_op | source)
XLA Modules:
  0.0 54.3 jit_solution(6063300599867733762)
XLA Ops:
  0.6 53.0 %attention_grad.1 = (bf16[128,512]{1,0:T(8,128)(2,1)S(1)}, bf16[128,128]{1,0:T(8,128)(2,1)S(1)}, bf16[128,128]{1,0:T(8,128)(2,1)S(1)}) custom-call(bf16[128,512]{1,0:T(8,128)(2,1)} %q_ref.1, bf16[128,128]{1,0:T(8,128)(2,1)} %k_ref.1, bf16[128,128]{1,0:T(8,128)(2,1)} %v_ref.1, bf16[128,512]{1,0:T(8,128)(2,1)} %o_ref.1, bf16[128,512]{1,0:T(8,128)(2,1)} %do_ref.1, ...), custom_call_target="tpu_custom_call" | custom-call | tf_op jit(solution)/shard_map/attention_grad/pallas_call | solution.py:493
  53.6 0.7 %hand_on.1 = (bf16[128,512]{1,0:T(8,128)(2,1)}, bf16[128,128]{1,0:T(8,128)(2,1)}, bf16[128,128]{1,0:T(8,128)(2,1)}) custom-call(bf16[128,512]{1,0:T(8,128)(2,1)S(1)} %get-tuple-element.6.a_ref, bf16[128,128]{1,0:T(8,128)(2,1)S(1)} %get-tuple-element.7.b_ref, bf16[128,128]{1,0:T(8,128)(2,1)S(1)} %get-tuple-element.8.c_ref), custom_call_target="tpu_custom_call" | custom-call | tf_op jit(solution)/shard_map/hand_on/pallas_call | solution.py:542

commit v6 on v5

--- a/solution.py
+++ b/solution.py
@@ -198,19 +198,19 @@
             (0, 3, 0, right), (0, 3, 1, right), (0, 1, 1, left), (0, 1, 0, left), (3, 2, 0, right), (1, 2, 1, left)
         )[n]
         return rcopy(
-            qx.at[:, half, src + 4 * u], qx.at[:, half, dst + 4 * u], ss.at[10 + n + 18 * u], xr.at[u, n], to
+            qx.at[:, half, src + 4 * u], qx.at[:, half, dst + 4 * u], ss.at[10 + u], xr.at[u, n], to
         )
 
     def zq_copy(half):
-        return rcopy(qx.at[:, half, 0], qx.at[:, half, 4], ss.at[34], cr.at[8 + half], partner)
+        return rcopy(qx.at[:, half, 0], qx.at[:, half, 4], ss.at[12], cr.at[8 + half], partner)
 
     def m_copy(d):
         return rcopy(sm.at[0], sm.at[d], ss.at[16], cr.at[2], dev(x - d, y, z, c))
 
-    mz_copy = rcopy(sm.at[0], sm.at[4], ss.at[35], cr.at[10], partner)
+    mz_copy = rcopy(sm.at[0], sm.at[4], ss.at[13], cr.at[10], partner)
 
     def m2_copy(d):
-        return rcopy(sm.at[4], sm.at[4 + d], ss.at[36], cr.at[11], dev(x - d, y, z, c))
+        return rcopy(sm.at[4], sm.at[4 + d], ss.at[14], cr.at[11], dev(x - d, y, z, c))
 
     def stage_full(s):
         z_copy(s).wait_recv()
@@ -254,12 +254,12 @@
         rows = pl.ds(64 * half, 64)
         got = cr.at[12 + half] if u else cr.at[4]
         return rcopy(
-            dqs.at[d + 4 * u, rows], qin.at[d + 4 * u, rows], ss.at[37 if u else 24], got, dev(x + d, y, z, c)
+            dqs.at[d + 4 * u, rows], qin.at[d + 4 * u, rows], ss.at[15 if u else 24], got, dev(x + d, y, z, c)
         )
 
     def rp_copy(half):
         rows = pl.ds(64 * half, 64)
-        return rcopy(qb.at[rows], qp.at[rows], ss.at[38], cr.at[14 + half], partner)
+        return rcopy(qb.at[rows], qp.at[rows], ss.at[28], cr.at[14 + half], partner)
 
     def share(half):
         rows = pl.ds(64 * half, 64)
@@ -425,21 +425,17 @@
     all_of(kv.at[c, rest, 0], ss.at[8]).wait()
     all_of(kv.at[c, :, rest], ss.at[9]).wait()
     for u in range(2):
-        for n in range(6):
-            x_copy(n, u).wait_send()
-    all_of(qx.at[:, :, 4], ss.at[34]).wait()
+        all_of(qx.at[:, :, pl.ds(1 + 4 * u, 3)], ss.at[10 + u]).wait()
+    all_of(qx.at[:, :, 4], ss.at[12]).wait()
     all_of(sm.at[rest], ss.at[16]).wait()
-    all_of(sm.at[4], ss.at[35]).wait()
-    all_of(sm.at[pl.ds(5, 3)], ss.at[36]).wait()
+    all_of(sm.at[4], ss.at[13]).wait()
+    all_of(sm.at[pl.ds(5, 3)], ss.at[14]).wait()
     all_of(qin.at[rest], cr.at[4]).wait()
     qsum = dqs[0].astype(F32)
     for d in (1, 2, 3):
         qsum = qsum + qin[d].astype(F32)
-    to_owner(3, own_sum(3))
-    to_owner(1, direct_sum(1))
-    to_owner(2, own_sum(2))
-    tot0[...] = direct_sum(0)
-    for half in range(2):
+
+    def to_partner(half):
         rows = pl.ds(64 * half, 64)
         all_of(qin.at[pl.ds(5, 3), rows], cr.at[12 + half]).wait()
         psum = dqs[4, rows].astype(F32)
@@ -447,6 +443,13 @@
             psum = psum + qin[4 + d, rows].astype(F32)
         qb[rows] = psum.astype(BF)
         rp_copy(half).start()
+
+    to_owner(3, own_sum(3))
+    to_owner(1, direct_sum(1))
+    to_partner(0)
+    to_owner(2, own_sum(2))
+    tot0[...] = direct_sum(0)
+    to_partner(1)
     all_of(zin.at[rest], cr.at[3]).wait()
     tot = tot0[...]
     for s in (1, 2, 3):
@@ -467,8 +470,8 @@
     all_of(rc, ss.at[22]).wait()
     all_of(zin.at[rest], ss.at[23]).wait()
     all_of(qin.at[rest], ss.at[24]).wait()
-    all_of(qin.at[pl.ds(5, 3)], ss.at[37]).wait()
-    all_of(qp, ss.at[38]).wait()
+    all_of(qin.at[pl.ds(5, 3)], ss.at[15]).wait()
+    all_of(qp, ss.at[28]).wait()
     low = c == 0
     sk.wait()
     gk_ref[...] = jnp.where(low, fin[0], fin[1])
@@ -527,7 +530,7 @@
             pltpu.VMEM((2, 128, 128), BF),
             pltpu.VMEM((4, 128), F32),
             pltpu.VMEM((1, 128), jnp.int32),
-            DMA((39,)), DMA((4,)), DMA((4, 4)), DMA((4,)), DMA((2, 6)), DMA((16,)), DMA((4,)), DMA((4, 4)), DMA((7,)),
+            DMA((29,)), DMA((4,)), DMA((4, 4)), DMA((4,)), DMA((2, 6)), DMA((16,)), DMA((4,)), DMA((4, 4)), DMA((7,)),
         ],
         compiler_params=pltpu.CompilerParams(
             collective_id=0, has_side_effects=True, vmem_limit_bytes=24 * 2**20

time: 54.5 us -> 54.4 us (level)
  no operation moved by 1% of the time
where the time goes in v6:
time: 54.4 us; the launch traced here: 54.2 us
  Pallas kernels  53.6 us (99%)
  between operations  0.64 us (1%)
    pallas_call x1, Pallas kernels, per_device(): pl.pallas_call(fused_kernel, out_shape=(jax.ShapeDtypeStruct((128, 512),...  52.9 us

profile of v6, /device:TPU:1, one launch (start us, length us, event | category | flops | bytes accessed | tf_op | source)
XLA Modules:
  0.0 54.2 jit_solution(9102818027867902790)
XLA Ops:
  0.6 52.9 %attention_grad.1 = (bf16[128,512]{1,0:T(8,128)(2,1)S(1)}, bf16[128,128]{1,0:T(8,128)(2,1)S(1)}, bf16[128,128]{1,0:T(8,128)(2,1)S(1)}) custom-call(bf16[128,512]{1,0:T(8,128)(2,1)} %q_ref.1, bf16[128,128]{1,0:T(8,128)(2,1)} %k_ref.1, bf16[128,128]{1,0:T(8,128)(2,1)} %v_ref.1, bf16[128,512]{1,0:T(8,128)(2,1)} %o_ref.1, bf16[128,512]{1,0:T(8,128)(2,1)} %do_ref.1, ...), custom_call_target="tpu_custom_call" | custom-call | tf_op jit(solution)/shard_map/attention_grad/pallas_call | solution.py:496
  53.5 0.7 %hand_on.1 = (bf16[128,512]{1,0:T(8,128)(2,1)}, bf16[128,128]{1,0:T(8,128)(2,1)}, bf16[128,128]{1,0:T(8,128)(2,1)}) custom-call(bf16[128,512]{1,0:T(8,128)(2,1)S(1)} %get-tuple-element.6.a_ref, bf16[128,128]{1,0:T(8,128)(2,1)S(1)} %get-tuple-element.7.b_ref, bf16[128,128]{1,0:T(8,128)(2,1)S(1)} %get-tuple-element.8.c_ref), custom_call_target="tpu_custom_call" | custom-call | tf_op jit(solution)/shard_map/hand_on/pallas_call | solution.py:545
